TPU v7x, 32 devices: a whole 2x2x4 slice. The times are simulated.
32 devices in a mesh: rep: 8 (over z, y), shard: 4 (over x, core).
Axes of the slice: x: 2, y: 2, z: 4, core: 2. Of those that a mesh axis runs over, the one named last changes fastest.
Arguments:
- tokens: bfloat16 [32, 512, 1024], P('rep', 'shard'), may hold values from -6 to 6
- enc_states: bfloat16 [32, 256, 1024], P(('rep', 'shard')), may hold values from -6 to 6
- cotangent: bfloat16 [32, 512, 1024], P('rep', 'shard'), may hold values from -6 to 6
- lengths: int32 [8, 4], P('rep'), may hold values from 1 to 512, 1280 in all within a row
- owner: int32 [8, 4], P('rep'), may hold values from 0 to 3, each once within a row
- attn_in: bfloat16 [6, 1024, 1024], P(None, 'shard'), may hold values from -0.1875 to 0.1875
- attn_out: bfloat16 [2, 1024, 1024], P(None, 'shard'), may hold values from -2 to 2
- attn_bias: bfloat16 [6, 1024], P(None, 'shard'), may hold values from -3 to 3
- norm_gain: bfloat16 [3, 1024], P(None, 'shard'), may hold values from 0.25 to 1.75
- norm_bias: bfloat16 [3, 1024], P(None, 'shard'), may hold values from -3 to 3
- mlp_in: bfloat16 [1024, 4096], P('shard'), may hold values from -0.1875 to 0.1875
- mlp_bias_in: bfloat16 [4096], P('shard'), may hold values from -3 to 3
- mlp_out: bfloat16 [4096, 1024], P('shard'), may hold values from -0.09375 to 0.09375
- mlp_bias_out: bfloat16 [1024], P('shard'), may hold values from -3 to 3
Outputs:
- out: bfloat16 [32, 512, 1024], P('rep', 'shard')
- grad_tokens: bfloat16 [32, 512, 1024], P('rep', 'shard')
- grad_enc: bfloat16 [32, 256, 1024], P(('rep', 'shard'))
- grad_attn_in: float32 [6, 1024, 1024], P(None, 'shard')
- grad_attn_out: float32 [2, 1024, 1024], P(None, 'shard')
- grad_attn_bias: float32 [6, 1024], P(None, 'shard')
- grad_norm_gain: float32 [3, 1024], P(None, 'shard')
- grad_norm_bias: float32 [3, 1024], P(None, 'shard')
- grad_mlp_in: float32 [1024, 4096], P('shard')
- grad_mlp_bias_in: float32 [4096], P('shard')
- grad_mlp_out: float32 [4096, 1024], P('shard')
- grad_mlp_bias_out: float32 [1024], P('shard')
Inputs may be any that keep to these rules, and one draw needn't show every extreme that they name: Row r holds the lengths of the 4 sequences of group r; they sum to 1280, and the longest of each row is 512. Each row is a permutation: sequence i of group r is handled at index owner[r, i] of shard, and its encoder states are block r * 4 + owner[r, i] of enc_states.
All inputs are finite; a program needn't handle non-finite values.
Results may differ from a plain program's by a relative error of at most 0.024.
The roundings to bfloat16 on the way count: a program that leaves them out, or rounds other values in their place, can miss the bound.
Values may be sent and summed in bfloat16 or wider, within the bound.
A program may use at most 256 MiB of HBM per device.

v0:
```python
import jax
import jax.numpy as jnp
from jax import lax
from jax.sharding import PartitionSpec as P

HEADS = 16
HEAD_DIM = 64


epsilon = 1e-05


def matmul(left, right):
    return jnp.dot(left, right, preferred_element_type=jnp.float32)


def contract_rows(left, right):
    return lax.dot_general(
        left, right, (((0,), (0,)), ((), ())), preferred_element_type=jnp.float32
    )


def contract_cols(left, right):
    return lax.dot_general(
        left, right, (((1,), (1,)), ((), ())), preferred_element_type=jnp.float32
    )


def layer_norm(features, norm_scale, norm_shift):
    center = features - jnp.mean(features, axis=-1, keepdims=True)
    spread = jnp.mean(center * center, axis=-1, keepdims=True)
    return center * lax.rsqrt(spread + epsilon) * norm_scale + norm_shift


def gelu_exact(features):
    return jax.nn.gelu(features, approximate=False)


def column_sum(matrix):
    return jnp.sum(matrix.astype(jnp.float32), axis=0)


def split_heads(matrix):
    width = min(4, HEADS)
    return jnp.moveaxis(matrix.reshape(matrix.shape[0], HEADS // width, width, HEAD_DIM), 1, 0)


def merge_heads(stacked):
    return jnp.moveaxis(stacked, 0, 1).reshape(stacked.shape[1], HEADS * HEAD_DIM)


def block_scores(query_block, key_group, offset, causal):
    scores = jnp.einsum(
        "qgd,kgd->gqk", query_block, key_group, preferred_element_type=jnp.float32
    ) * HEAD_DIM ** (-0.5)
    if causal:
        query_pos = offset + jnp.arange(query_block.shape[0], dtype=jnp.int32)
        key_pos = jnp.arange(key_group.shape[0], dtype=jnp.int32)
        scores = jnp.where(key_pos[None, None, :] <= query_pos[None, :, None], scores, -jnp.inf)
    return scores


def attention_forward(queries, keys, values, causal):
    row_count = queries.shape[0]
    block_rows = min(512, row_count)
    block_count = row_count // block_rows
    offsets = jnp.arange(block_count, dtype=jnp.int32) * block_rows

    def per_group(operands):
        query_group, key_group, value_group = operands
        width = query_group.shape[1]
        query_blocks = query_group.reshape(block_count, block_rows, width, HEAD_DIM)

        def per_block(block_items):
            query_block, offset = block_items
            scores = block_scores(query_block, key_group, offset, causal)
            peak = jnp.max(scores, axis=-1, keepdims=True)
            log_total = peak + jnp.log(jnp.sum(jnp.exp(scores - peak), axis=-1, keepdims=True))
            weights_low = jnp.exp(scores - log_total).astype(jnp.bfloat16)
            context = jnp.einsum(
                "gqk,kgd->qgd", weights_low, value_group, preferred_element_type=jnp.float32
            )
            return (context.astype(jnp.bfloat16), log_total)

        context, log_totals = lax.map(per_block, (query_blocks, offsets))
        return (context.reshape(row_count, width, HEAD_DIM), log_totals)

    context, log_totals = lax.map(
        per_group, (split_heads(queries), split_heads(keys), split_heads(values))
    )
    return (merge_heads(context), log_totals)


def attention_backward(queries, keys, values, log_totals, context_grad, causal):
    row_count = queries.shape[0]
    block_rows = min(512, row_count)
    block_count = row_count // block_rows
    offsets = jnp.arange(block_count, dtype=jnp.int32) * block_rows
    scale = HEAD_DIM ** (-0.5)

    def per_group(operands):
        query_group, key_group, value_group, grad_group, total_group = operands
        width = query_group.shape[1]
        query_blocks = query_group.reshape(block_count, block_rows, width, HEAD_DIM)
        grad_blocks = grad_group.reshape(block_count, block_rows, width, HEAD_DIM)

        def per_block(accumulated, block_items):
            key_grad, value_grad = accumulated
            query_block, grad_block, log_total, offset = block_items
            scores = block_scores(query_block, key_group, offset, causal)
            weights_full = jnp.exp(scores - log_total)
            weights_low = weights_full.astype(jnp.bfloat16)
            value_grad = value_grad + jnp.einsum(
                "gqk,qgd->kgd", weights_low, grad_block, preferred_element_type=jnp.float32
            )
            weight_grad = jnp.einsum(
                "qgd,kgd->gqk", grad_block, value_group, preferred_element_type=jnp.float32
            )
            row_dot = jnp.sum(weights_full * weight_grad, axis=-1, keepdims=True)
            score_grad = (weights_full * (weight_grad - row_dot)).astype(jnp.bfloat16)
            query_grad = (
                jnp.einsum(
                    "gqk,kgd->qgd", score_grad, key_group, preferred_element_type=jnp.float32
                )
                * scale
            )
            key_grad = (
                key_grad
                + jnp.einsum(
                    "gqk,qgd->kgd", score_grad, query_block, preferred_element_type=jnp.float32
                )
                * scale
            )
            return ((key_grad, value_grad), query_grad)

        empty_grad = jnp.zeros(key_group.shape, jnp.float32)
        (key_grad, value_grad), query_grad = lax.scan(
            per_block, (empty_grad, empty_grad), (query_blocks, grad_blocks, total_group, offsets)
        )
        return (query_grad.reshape(row_count, width, HEAD_DIM), key_grad, value_grad)

    query_grad, key_grad, value_grad = lax.map(
        per_group,
        (
            split_heads(queries),
            split_heads(keys),
            split_heads(values),
            split_heads(context_grad),
            log_totals,
        ),
    )
    return (merge_heads(query_grad), merge_heads(key_grad), merge_heads(value_grad))


def local(
    tokens,
    enc_states,
    cotangent,
    lengths,
    owner,
    attn_in,
    attn_out,
    attn_bias,
    norm_gain,
    norm_bias,
    mlp_in,
    mlp_bias_in,
    mlp_out,
    mlp_bias_out,
):
    groups = lax.axis_size("shard")
    my_index = lax.axis_index("shard")
    owner_row = owner[0]
    slot_ids = jnp.arange(groups, dtype=jnp.int32)
    matches = owner_row[None, :] == slot_ids[:, None]
    sequence_at = jnp.sum(jnp.where(matches, slot_ids[None, :], 0), axis=1)
    my_sequence = jnp.sum(jnp.where(slot_ids == my_index, sequence_at, 0))
    my_length = jnp.sum(jnp.where(slot_ids == my_sequence, lengths[0], 0))
    sent_tokens = jnp.take(tokens, sequence_at, axis=0)
    sent_grads = jnp.take(cotangent, sequence_at, axis=0)
    got_tokens, got_grads = (
        lax.all_to_all(sent_tokens, "shard", split_axis=0, concat_axis=1, tiled=True),
        lax.all_to_all(sent_grads, "shard", split_axis=0, concat_axis=1, tiled=True),
    )
    inputs = got_tokens[0]
    row_count = inputs.shape[0]
    row_mask = (jnp.arange(row_count, dtype=jnp.int32) < my_length).astype(jnp.float32)[:, None]
    encoder = enc_states[0]
    full_in, full_out, full_bias, full_gain, full_shift = (
        lax.all_gather(attn_in, "shard", axis=1, tiled=True),
        lax.all_gather(attn_out, "shard", axis=1, tiled=True),
        lax.all_gather(attn_bias, "shard", axis=1, tiled=True),
        lax.all_gather(norm_gain, "shard", axis=1, tiled=True),
        lax.all_gather(norm_bias, "shard", axis=1, tiled=True),
    )
    bias_rows = full_bias.astype(jnp.float32)
    gain_rows = full_gain.astype(jnp.float32)
    shift_rows = full_shift.astype(jnp.float32)
    projected = jnp.einsum("rd,wde->wre", inputs, full_in[:3], preferred_element_type=jnp.float32)
    queries = (projected[0] + bias_rows[0]).astype(jnp.bfloat16)
    keys = projected[1].astype(jnp.bfloat16)
    values = (projected[2] + bias_rows[1]).astype(jnp.bfloat16)
    context, log_totals = attention_forward(queries, keys, values, True)
    first_sum = inputs.astype(jnp.float32) + (matmul(context, full_out[0]) + bias_rows[2])
    first_norm = layer_norm(first_sum, gain_rows[0], shift_rows[0])
    first_low = first_norm.astype(jnp.bfloat16)
    cross_queries = (matmul(first_low, full_in[3]) + bias_rows[3]).astype(jnp.bfloat16)
    cross_projected = jnp.einsum(
        "rd,wde->wre", encoder, full_in[4:6], preferred_element_type=jnp.float32
    )
    cross_keys = cross_projected[0].astype(jnp.bfloat16)
    cross_values = (cross_projected[1] + bias_rows[4]).astype(jnp.bfloat16)
    cross_context, cross_totals = attention_forward(cross_queries, cross_keys, cross_values, False)
    second_sum = first_norm + (matmul(cross_context, full_out[1]) + bias_rows[5])
    second_norm = layer_norm(second_sum, gain_rows[1], shift_rows[1])
    second_low = second_norm.astype(jnp.bfloat16)
    up_full, up_bias, down_full, down_bias = (
        lax.all_gather(mlp_in, "shard", axis=0, tiled=True),
        lax.all_gather(mlp_bias_in, "shard", axis=0, tiled=True),
        lax.all_gather(mlp_out, "shard", axis=0, tiled=True),
        lax.all_gather(mlp_bias_out, "shard", axis=0, tiled=True),
    )
    hidden_pre = matmul(second_low, up_full) + up_bias.astype(jnp.float32)
    hidden_low = gelu_exact(hidden_pre).astype(jnp.bfloat16)
    third_sum = second_norm + (matmul(hidden_low, down_full) + down_bias.astype(jnp.float32))
    result = (layer_norm(third_sum, gain_rows[2], shift_rows[2]) * row_mask).astype(jnp.bfloat16)
    back_blocks = lax.all_to_all(result[None], "shard", split_axis=1, concat_axis=0, tiled=True)
    output = jnp.take(back_blocks, owner_row, axis=0)
    out_grad = got_grads[0].astype(jnp.float32) * row_mask
    third_grad, third_gain_grad, third_shift_grad = jax.vjp(
        layer_norm, third_sum, gain_rows[2], shift_rows[2]
    )[1](out_grad)
    up_back, down_back = (
        lax.all_gather(mlp_in, "shard", axis=0, tiled=True),
        lax.all_gather(mlp_out, "shard", axis=0, tiled=True),
    )
    down_grad_in = third_grad.astype(jnp.bfloat16)
    grad_down = contract_rows(hidden_low, down_grad_in)
    grad_down_bias = column_sum(down_grad_in)
    hidden_grad = contract_cols(down_grad_in, down_back)
    hidden_pre_grad = jax.vjp(gelu_exact, hidden_pre)[1](hidden_grad)[0].astype(jnp.bfloat16)
    grad_up = contract_rows(second_low, hidden_pre_grad)
    grad_up_bias = column_sum(hidden_pre_grad)
    second_norm_grad = third_grad + contract_cols(hidden_pre_grad, up_back)
    mlp_parts = (
        lax.psum_scatter(
            grad_up.astype(jnp.bfloat16), "shard", scatter_dimension=0, tiled=True
        ).astype(jnp.float32),
        lax.psum_scatter(
            grad_up_bias.astype(jnp.bfloat16), "shard", scatter_dimension=0, tiled=True
        ).astype(jnp.float32),
        lax.psum_scatter(
            grad_down.astype(jnp.bfloat16), "shard", scatter_dimension=0, tiled=True
        ).astype(jnp.float32),
        lax.psum_scatter(
            grad_down_bias.astype(jnp.bfloat16), "shard", scatter_dimension=0, tiled=True
        ).astype(jnp.float32),
    )
    second_grad, second_gain_grad, second_shift_grad = jax.vjp(
        layer_norm, second_sum, gain_rows[1], shift_rows[1]
    )[1](second_norm_grad)
    in_back, out_back = (
        lax.all_gather(attn_in, "shard", axis=1, tiled=True),
        lax.all_gather(attn_out, "shard", axis=1, tiled=True),
    )
    cross_out_grad = second_grad.astype(jnp.bfloat16)
    grad_cross_out = contract_rows(cross_context, cross_out_grad)
    grad_cross_out_bias = column_sum(cross_out_grad)
    cross_context_grad = contract_cols(cross_out_grad, out_back[1]).astype(jnp.bfloat16)
    cross_query_grad, cross_key_grad, cross_value_grad = attention_backward(
        cross_queries, cross_keys, cross_values, cross_totals, cross_context_grad, False
    )
    cross_query_low = cross_query_grad.astype(jnp.bfloat16)
    cross_key_low = cross_key_grad.astype(jnp.bfloat16)
    cross_value_low = cross_value_grad.astype(jnp.bfloat16)
    grad_cross_query = contract_rows(first_low, cross_query_low)
    grad_cross_query_bias = column_sum(cross_query_low)
    grad_cross_key = contract_rows(encoder, cross_key_low)
    grad_cross_value = contract_rows(encoder, cross_value_low)
    grad_cross_value_bias = column_sum(cross_value_low)
    encoder_grad = (
        contract_cols(cross_key_low, in_back[4]) + contract_cols(cross_value_low, in_back[5])
    ).astype(jnp.bfloat16)
    first_norm_grad = second_grad + contract_cols(cross_query_low, in_back[3])
    first_grad, first_gain_grad, first_shift_grad = jax.vjp(
        layer_norm, first_sum, gain_rows[0], shift_rows[0]
    )[1](first_norm_grad)
    self_out_grad = first_grad.astype(jnp.bfloat16)
    grad_self_out = contract_rows(context, self_out_grad)
    grad_self_out_bias = column_sum(self_out_grad)
    context_grad = contract_cols(self_out_grad, out_back[0]).astype(jnp.bfloat16)
    query_grad, key_grad, value_grad = attention_backward(
        queries, keys, values, log_totals, context_grad, True
    )
    query_low = query_grad.astype(jnp.bfloat16)
    key_low = key_grad.astype(jnp.bfloat16)
    value_low = value_grad.astype(jnp.bfloat16)
    grad_query = contract_rows(inputs, query_low)
    grad_query_bias = column_sum(query_low)
    grad_key = contract_rows(inputs, key_low)
    grad_value = contract_rows(inputs, value_low)
    grad_value_bias = column_sum(value_low)
    input_grad = (
        first_grad
        + contract_cols(query_low, in_back[0])
        + contract_cols(key_low, in_back[1])
        + contract_cols(value_low, in_back[2])
    ).astype(jnp.bfloat16)
    grad_blocks = lax.all_to_all(input_grad[None], "shard", split_axis=1, concat_axis=0, tiled=True)
    grad_tokens = jnp.take(grad_blocks, owner_row, axis=0)
    grad_in_full = jnp.stack(
        [grad_query, grad_key, grad_value, grad_cross_query, grad_cross_key, grad_cross_value]
    )
    grad_out_full = jnp.stack([grad_self_out, grad_cross_out])
    grad_bias_full = jnp.stack(
        [
            grad_query_bias,
            grad_value_bias,
            grad_self_out_bias,
            grad_cross_query_bias,
            grad_cross_value_bias,
            grad_cross_out_bias,
        ]
    )
    grad_gain_full = jnp.stack([first_gain_grad, second_gain_grad, third_gain_grad])
    grad_shift_full = jnp.stack([first_shift_grad, second_shift_grad, third_shift_grad])
    attn_parts = (
        lax.psum_scatter(
            grad_in_full.astype(jnp.bfloat16), "shard", scatter_dimension=1, tiled=True
        ).astype(jnp.float32),
        lax.psum_scatter(
            grad_out_full.astype(jnp.bfloat16), "shard", scatter_dimension=1, tiled=True
        ).astype(jnp.float32),
        lax.psum_scatter(
            grad_bias_full.astype(jnp.bfloat16), "shard", scatter_dimension=1, tiled=True
        ).astype(jnp.float32),
        lax.psum_scatter(
            grad_gain_full.astype(jnp.bfloat16), "shard", scatter_dimension=1, tiled=True
        ).astype(jnp.float32),
        lax.psum_scatter(
            grad_shift_full.astype(jnp.bfloat16), "shard", scatter_dimension=1, tiled=True
        ).astype(jnp.float32),
    )
    summed = (
        lax.psum(attn_parts[0].astype(jnp.bfloat16), "rep").astype(jnp.float32),
        lax.psum(attn_parts[1].astype(jnp.bfloat16), "rep").astype(jnp.float32),
        lax.psum(attn_parts[2].astype(jnp.bfloat16), "rep").astype(jnp.float32),
        lax.psum(attn_parts[3].astype(jnp.bfloat16), "rep").astype(jnp.float32),
        lax.psum(attn_parts[4].astype(jnp.bfloat16), "rep").astype(jnp.float32),
        lax.psum(mlp_parts[0].astype(jnp.bfloat16), "rep").astype(jnp.float32),
        lax.psum(mlp_parts[1].astype(jnp.bfloat16), "rep").astype(jnp.float32),
        lax.psum(mlp_parts[2].astype(jnp.bfloat16), "rep").astype(jnp.float32),
        lax.psum(mlp_parts[3].astype(jnp.bfloat16), "rep").astype(jnp.float32),
    )
    return (
        output,
        grad_tokens,
        encoder_grad[None],
        summed[0],
        summed[1],
        summed[2],
        summed[3],
        summed[4],
        summed[5],
        summed[6],
        summed[7],
        summed[8],
    )


def solution(mesh):
    placed = (
        P("rep", "shard", None),
        P(("rep", "shard"), None, None),
        P("rep", "shard", None),
        P("rep", None),
        P("rep", None),
        P(None, "shard", None),
        P(None, "shard", None),
        P(None, "shard"),
        P(None, "shard"),
        P(None, "shard"),
        P("shard", None),
        P("shard"),
        P("shard", None),
        P("shard"),
    )
    return jax.shard_map(
        local,
        mesh=mesh,
        in_specs=placed,
        out_specs=(
            P("rep", "shard", None),
            P("rep", "shard", None),
            P(("rep", "shard"), None, None),
            P(None, "shard", None),
            P(None, "shard", None),
            P(None, "shard"),
            P(None, "shard"),
            P(None, "shard"),
            P("shard", None),
            P("shard"),
            P("shard", None),
            P("shard"),
        ),
        check_vma=False,
    )
```

profile of v0, /device:TPU:0, one launch (start us, length us, event | category | flops | bytes accessed | tf_op | source)
XLA Modules:
  0.0 1016.1 jit_solution(13245577582402485065)
XLA Ops:
  13.7 4.4 all-to-all-start
  18.6 23.0 %all_gather.32 = bf16[6,1024]{1,0:T(8,128)(2,1)S(1)} all-gather(bf16[6,256]{1,0:T(8,128)(2,1)S(1)} %copy-done.57), channel_id=1, replica_groups=mesh['rep'=8,'shard'=4] {'shard'}, dimensions={1}, use_global_device_ids=true | all-gather | bytes 15360 | tf_op jit(solution)/shard_map/all_gather | solution.py:192
  41.6 5.2 all_gather.34
  46.8 5.2 all_gather.35
  52.0 5.2 all_gather.37
  57.1 5.1 all-gather
  64.4 4.2 all-to-all-start.2
  68.9 44.5 %all-gather.6.cloned.1.call-done = bf16[6,1024,1024]{2,1,0:T(8,128)(2,1)} async-done(((bf16[6,256,1024]{2,1,0:T(8,128)(2,1)}), bf16[6,1024,1024]{2,1,0:T(8,128)(2,1)}) %all-gather.6.cloned.1.call-update) | async-done | bytes 12582928 | tf_op jit(solution)/shard_map/all_gather | solution.py:190
  113.4 5.5 fusion.102
  122.3 4.0 convolution_bitcast_fusion.1
  127.6 2.9 copy.106
  130.5 2.9 copy.107
  133.9 2.9 fusion.125
  138.2 19.4 %while.46 = (s32[]{:T(128)}, bf16[4,512,4,64]{1,3,2,0:T(8,128)(2,1)}, f32[4,1,4,512,1]{3,2,4,1,0:T(4,128)S(1)}, bf16[4,512,4,64]{1,3,2,0:T(8,128)(2,1)}, bf16[4,...) while((s32[]{:T(128)}, bf16[4,512,4,64]{1,3,2,0:T(8,128)(2,1)}, ...), condition=%wide.region_4.6_spmd, body=%wide.region_1.5_spmd.sunk | while | flops 280360960 | bytes 14747729 | solution.py:88
  140.1 2.9 fusion.229
  144.9 2.9 fusion.229
  149.8 2.9 fusion.229
  154.6 2.9 fusion.229
  157.6 4.8 fusion.156
  163.8 4.1 add_convert_fusion.2
  169.8 5.8 while.47
  175.7 4.5 fusion.157
  182.0 28.5 %all-gather.10.cloned.1.call-done = bf16[1024,4096]{1,0:T(8,128)(2,1)} async-done(((bf16[256,4096]{1,0:T(8,128)(2,1)}), bf16[1024,4096]{1,0:T(8,128)(2,1)}) %all-gather.10.cloned.1.call-update) | async-done | bytes 8388624 | tf_op jit(solution)/shard_map/all_gather | solution.py:218
  210.4 28.3 %multiply_convert_fusion.2 = (bf16[512,4096]{1,0:T(8,128)(2,1)}, f32[512,4096]{1,0:T(8,128)}, f32[512,4096]{1,0:T(8,128)}) fusion(f32[4096]{0:T(1024)S(1)} %convert_element_type.296, bf16[1024,4096]{1,0:T(8,128)(2,1)} %all-gather.10.cloned.1.call-done, f32[512,1024]{1,0:T(8,128)} %copy-done.13, f32[1024]{0:T(1024)S(1)} %bitcast.481, ...), kind=kOutput, calls=%fused_computation.122 | convolution fusion | flops 4436000768 | bytes 31485952 | tf_op jit(solution)/shard_map/dot_general | solution.py:14
  238.8 31.4 %all-gather.12.cloned.1.call-done = bf16[4096,1024]{1,0:T(8,128)(2,1)} async-done(((bf16[1024,1024]{1,0:T(8,128)(2,1)}), bf16[4096,1024]{1,0:T(8,128)(2,1)}) %all-gather.12.cloned.1.call-update) | async-done | bytes 8388624 | tf_op jit(solution)/shard_map/all_gather | solution.py:220
  270.2 9.9 fusion.158
  280.5 2.6 multiply_reduce_fusion.4
  283.1 3.3 fusion.150
  287.2 14.4 %fusion.145 = (bf16[4096]{0:T(1024)(128)(2,1)}, bf16[512,4096]{1,0:T(8,128)(2,1)S(1)}) fusion(f32[512,4096]{1,0:T(8,128)} %get-tuple-element.378, f32[512,4096]{1,0:T(8,128)} %get-tuple-element.409, f32[4096]{0:T(1024)S(1)} %convert_element_type.296, bf16[512,1024]{1,0:T(8,128)(2,1)S(1)} %get-tuple-element.364, ...), kind=kOutput, calls=%fused_computation.264 | convolution fusion | flops 4328517632 | bytes 30433280 | tf_op jit(solution)/shard_map/dot_general | solution.py:24
  301.6 9.1 multiply_reduce_fusion.5
  313.4 2.6 convert_bitcast_fusion
  321.0 23.6 %while.48 = (s32[]{:T(128)}, bf16[4,512,4,64]{1,3,2,0:T(8,128)(2,1)}, bf16[4,256,4,64]{1,3,2,0:T(8,128)(2,1)}, bf16[4,256,4,64]{1,3,2,0:T(8,128)(2,1)}, bf16[4,2...) while((s32[]{:T(128)}, ...), condition=%wide.region_23.25_spmd, body=%wide.region_21.24_spmd.sunk | while | flops 339933184 | bytes 26653856 | solution.py:142
  344.6 5.4 multiply_reduce_fusion.6
  358.3 9.2 convolution_convert_fusion.2
  368.8 9.0 convolution_convert_fusion.1
  379.0 2.9 fusion.120
  386.1 40.0 %while.49 = (s32[]{:T(128)}, bf16[4,512,4,64]{1,3,2,0:T(8,128)(2,1)}, bf16[4,512,4,64]{1,3,2,0:T(8,128)(2,1)}, bf16[4,512,4,64]{1,3,2,0:T(8,128)(2,1)}, bf16[4,5...) while((s32[]{:T(128)}, ...), condition=%wide.region_28.30_spmd, body=%wide.region_26.29_spmd.sunk | while | flops 687339520 | bytes 52753624 | solution.py:142
  397.5 2.5 multiply_reduce_fusion.18
  407.4 2.5 multiply_reduce_fusion.18
  417.6 2.6 multiply_reduce_fusion.18
  426.1 4.7 bitcast_dynamic-update-slice_fusion.7
  430.8 2.6 bitcast_dynamic-update-slice_fusion.6
  433.4 4.0 bitcast_dynamic-update-slice_fusion.5
  437.5 2.9 bitcast_dynamic-update-slice_fusion.4
  452.3 23.5 %reduce-scatter.18.cloned.1.call-done = bf16[256,4096]{1,0:T(8,128)(2,1)} async-done(((bf16[1024,4096]{1,0:T(8,128)(2,1)}), bf16[256,4096]{1,0:T(8,128)(2,1)}) %reduce-scatter.18.cloned.1.call-update) | async-done | bytes 2097168 | tf_op jit(solution)/shard_map/reduce_scatter | solution.py:246
  475.8 74.3 %reduce-scatter.20.cloned.1.call-done = bf16[1024,1024]{1,0:T(8,128)(2,1)} async-done(((bf16[4096,1024]{1,0:T(8,128)(2,1)}), bf16[1024,1024]{1,0:T(8,128)(2,1)}) %reduce-scatter.20.cloned.1.call-update) | async-done | bytes 2097168 | tf_op jit(solution)/shard_map/reduce_scatter | solution.py:252
  550.2 101.8 %reduce-scatter.12.cloned.1.call-done = bf16[6,256,1024]{2,1,0:T(8,128)(2,1)} async-done(((bf16[6,1024,1024]{2,1,0:T(8,128)(2,1)}), bf16[6,256,1024]{2,1,0:T(8,128)(2,1)}) %reduce-scatter.12.cloned.1.call-update) | async-done | bytes 3145744 | tf_op jit(solution)/shard_map/reduce_scatter | solution.py:328
  653.2 2.9 fusion.108
  656.1 3.4 fusion.107
  659.5 3.2 fusion.121
  664.8 7.0 reduce.33
  673.8 3.5 all-to-all-start.3
  679.3 2.8 copy.137
  682.1 7.8 reduce.34
  689.9 3.8 reshape.433
  693.7 4.3 all-to-all-start.1
  698.0 20.2 %all-reduce.4 = (bf16[4096]{0:T(1024)(128)(2,1)S(1)}, bf16[1024]{0:T(1024)(128)(2,1)S(1)}) all-reduce(bf16[4096]{0:T(1024)(128)(2,1)S(1)} %copy-done.55, bf16[1024]{0:T(1024)(128)(2,1)S(1)} %copy-done.54), channel_id=8, replica_groups=mesh['rep'=8,'shard'=4] {'shard'}, use_global_device_ids=true, to_apply=%region_54.56.clone | all-reduce | flops 5120 | bytes 20480
  720.6 3.2 fusion.124
  725.7 39.4 %all-reduce.2 = (bf16[6,256]{1,0:T(8,128)(2,1)S(1)}, bf16[3,256]{1,0:T(4,128)(2,1)S(1)}, bf16[3,256]{1,0:T(4,128)(2,1)S(1)}, bf16[1024]{0:T(1024)(128)(2,1)S(1)}, bf16[256]{0:T(256)(128)(2,1)S(1)}) all-reduce(bf16[6,256]{1,0:T(8,128)(2,1)} %reduce-scatter.16.cloned.1.call-done, ...), channel_id=1, replica_groups=mesh['rep'=8,'shard'=4] {'rep'}, use_global_device_ids=true, to_apply=%region_40.42 | all-reduce | flops 4352 | bytes 17408 | tf_op jit(solution)/shard_map/psum | solution.py:347
  769.4 2.6 reshape.434
  776.9 220.0 %all-reduce.7.cloned.1.call-done = (bf16[6,256,1024]{2,1,0:T(8,128)(2,1)}, bf16[2,256,1024]{2,1,0:T(8,128)(2,1)}, bf16[256,4096]{1,0:T(8,128)(2,1)}, bf16[1024,1024]{1,0:T(8,128)(2,1)}) async-done(((bf16[6,256,1024]{2,1,0:T(8,128)(2,1)}, bf16[2,256,1024]{2,1,0:T(8,128)(2,1)}, bf16[256,4096]{1,0:T(8,128)(2,1)}, bf16[1024,1024]{1,0:T(8,128)(2,1)}), (bf16[6,256,1024]{2,1,0:T(8,128)(2,1)}, ...) | async-done | bytes 8388624 | tf_op jit(solution)/shard_map/psum | solution.py:345
  996.9 5.5 convert_element_type.329
  1002.4 2.5 convert_element_type.343
  1004.9 2.5 convert_element_type.346
  (410 shorter events, 146.2 us)
Async XLA Ops:
  7.2 3.6 copy-start
  7.2 106.2 %all-gather.6.cloned.1.call-start = ((), (), s32[]{:S(2)}) async-start(), calls=%async_computation.11 | async-start | bytes 15728640 | tf_op jit(solution)/shard_map/all_gather | solution.py:190
  7.9 149.6 %all-gather.8.cloned.1.call-start = ((), (), s32[]{:S(2)}) async-start(), calls=%async_computation.12 | async-start | bytes 5242880 | tf_op jit(solution)/shard_map/all_gather | solution.py:191
  8.7 2.7 copy-start.35
  8.7 201.7 %all-gather.10.cloned.1.call-start = ((), (), s32[]{:S(2)}) async-start(), calls=%async_computation.13 | async-start | bytes 10485760 | tf_op jit(solution)/shard_map/all_gather | solution.py:218
  13.6 5.0 copy-start.57
  13.6 28.0 %copy-start.60 = (bf16[3,256]{1,0:T(4,128)(2,1)S(1)}, bf16[3,256]{1,0:T(4,128)(2,1)}, u32[]{:S(2)}) copy-start(bf16[3,256]{1,0:T(4,128)(2,1)} %param.32) | copy-start | bytes 4612
  13.6 33.2 %copy-start.61 = (bf16[3,256]{1,0:T(4,128)(2,1)S(1)}, bf16[3,256]{1,0:T(4,128)(2,1)}, u32[]{:S(2)}) copy-start(bf16[3,256]{1,0:T(4,128)(2,1)} %param.33) | copy-start | bytes 4612
  13.6 38.3 %copy-start.62 = (bf16[1024]{0:T(1024)(128)(2,1)S(1)}, bf16[1024]{0:T(1024)(128)(2,1)}, u32[]{:S(2)}) copy-start(bf16[1024]{0:T(1024)(128)(2,1)} %param.35) | copy-start | bytes 6148
  13.6 43.5 %copy-start.64 = (bf16[256]{0:T(256)(128)(2,1)S(1)}, bf16[256]{0:T(256)(128)(2,1)}, u32[]{:S(2)}) copy-start(bf16[256]{0:T(256)(128)(2,1)} %param.37) | copy-start | bytes 1540
  13.7 48.6 %copy-start.65 = (s32[1,4]{1,0:T(1,128)S(1)}, s32[1,4]{1,0:T(1,128)}, u32[]{:S(2)}) copy-start(s32[1,4]{1,0:T(1,128)} %param.27) | copy-start | bytes 52
  13.7 50.7 %all-to-all-start = ((bf16[4,128,1024]{2,1,0:T(8,128)(2,1)}), bf16[4,128,1024]{2,1,0:T(8,128)(2,1)S(1)}, u32[]{:S(2)}, u32[]{:S(2)}) async-start(bf16[4,128,1024]{2,1,0:T(8,128)(2,1)} %get-tuple-element.402), calls=%async_computation | async-start | bytes 2097152 | tf_op jit(solution)/shard_map/all_to_all | solution.py:182
  18.0 252.2 %all-gather.12.cloned.1.call-start = ((), (), s32[]{:S(2)}) async-start(), calls=%async_computation.14 | async-start | bytes 10485760 | tf_op jit(solution)/shard_map/all_gather | solution.py:220
  64.3 111.4 %copy-start.58 = (f32[1,1024]{1,0:T(1,128)}, f32[1,1024]{1,0:T(1,128)S(1)}, u32[]{:S(2)}) copy-start(f32[1,1024]{1,0:T(1,128)S(1)} %get-tuple-element.398) | copy-start | bytes 12292
  64.4 54.5 %copy-start.36 = (bf16[4,128,1024]{2,1,0:T(8,128)(2,1)}, bf16[4,128,1024]{2,1,0:T(8,128)(2,1)S(1)}, u32[]{:S(2)}) copy-start(bf16[4,128,1024]{2,1,0:T(8,128)(2,1)S(1)} %all-to-all-done) | copy-start | bytes 3145732
  64.4 216.0 %all-to-all-start.2 = ((bf16[4,128,1024]{2,1,0:T(8,128)(2,1)}), bf16[4,128,1024]{2,1,0:T(8,128)(2,1)}, u32[]{:S(2)}, u32[]{:S(2)}) async-start(bf16[4,128,1024]{2,1,0:T(8,128)(2,1)} %get-tuple-element.401), calls=%async_computation.2 | async-start | bytes 2097152 | tf_op jit(solution)/shard_map/all_to_all | solution.py:183
  68.7 383.7 %reduce-scatter.14.cloned.1.call-start = ((), (), s32[]{:S(2)}) async-start(), calls=%async_computation.16 | async-start | bytes 5242880 | tf_op jit(solution)/shard_map/reduce_scatter | solution.py:331
  133.9 2.9 copy-start.17
  157.5 4.8 copy-start.2
  157.5 4.8 copy-start.4
  157.5 4.8 copy-start.51
  162.7 5.1 copy-start.52
  175.7 4.5 copy-start.6
  175.7 4.5 copy-start.18
  175.7 4.5 copy-start.46
  287.2 14.4 %copy-start.38 = (bf16[512,1024]{1,0:T(8,128)(2,1)}, bf16[512,1024]{1,0:T(8,128)(2,1)S(1)}, u32[]{:S(2)}) copy-start(bf16[512,1024]{1,0:T(8,128)(2,1)S(1)} %get-tuple-element.364) | copy-start | bytes 3145732
  287.2 14.4 %copy-start.14 = (f32[512,1024]{1,0:T(8,128)S(1)}, f32[512,1024]{1,0:T(8,128)}, u32[]{:S(2)}) copy-start(f32[512,1024]{1,0:T(8,128)} %copy-done.13) | copy-start | bytes 6291460
  301.6 9.1 copy-start.69
  311.4 4.6 copy-start.16
  313.4 2.6 copy-start.63
  318.3 2.7 copy-start.7
  344.6 5.4 copy-start.53
  344.6 5.4 copy-start.9
  356.7 119.1 %reduce-scatter.18.cloned.1.call-start = ((), (), s32[]{:S(2)}) async-start(), calls=%async_computation.18 | async-start | bytes 10485760 | tf_op jit(solution)/shard_map/reduce_scatter | solution.py:246
  367.5 182.7 %reduce-scatter.20.cloned.1.call-start = ((), (), s32[]{:S(2)}) async-start(), calls=%async_computation.19 | async-start | bytes 10485760 | tf_op jit(solution)/shard_map/reduce_scatter | solution.py:252
  377.8 274.2 %reduce-scatter.12.cloned.1.call-start = ((), (), s32[]{:S(2)}) async-start(), calls=%async_computation.15 | async-start | bytes 15728640 | tf_op jit(solution)/shard_map/reduce_scatter | solution.py:328
  382.8 3.2 copy-start.3
  382.8 3.2 copy-start.5
  426.1 4.7 copy-start.37
  426.1 4.7 copy-start.44
  433.4 4.0 copy-start.10
  433.4 4.0 copy-start.26
  433.4 4.0 copy-start.59
  437.4 2.9 copy-start.33
  437.5 2.9 copy-start.49
  444.6 2.3 copy-start.56
  444.6 3.2 copy-start.23
  444.7 279.1 %reduce-scatter.22.cloned.1.call-start = ((), (), s32[]{:S(2)}) async-start(), calls=%async_computation.20 | async-start | bytes 327680
  449.8 274.9 %reduce-scatter.24.cloned.1.call-start = ((), (), s32[]{:S(2)}) async-start(), calls=%async_computation.21 | async-start | bytes 327680
  450.8 274.9 %reduce-scatter.16.cloned.1.call-start = ((), (), s32[]{:S(2)}) async-start(), calls=%async_computation.17 | async-start | bytes 20480 | tf_op jit(solution)/shard_map/reduce_scatter | solution.py:334
  452.1 544.8 %all-reduce.7.cloned.1.call-start = ((), (), s32[]{:S(2)}) async-start(), calls=%async_computation.22 | async-start | bytes 16777216 | tf_op jit(solution)/shard_map/psum | solution.py:345
  656.1 3.4 copy-start.12
  671.8 5.5 copy-start.68
  673.8 19.8 %all-to-all-start.3 = ((bf16[4,2,65536]{2,1,0:T(2,128)(2,1)}), bf16[4,2,65536]{2,1,0:T(2,128)(2,1)S(1)}, u32[]{:S(2)}, u32[]{:S(2)}) async-start(bf16[4,2,65536]{2,1,0:T(2,128)(2,1)} %reshape.435), calls=%async_computation.3 | async-start | bytes 2097152 | tf_op jit(solution)/shard_map/all_to_all | solution.py:309
  689.9 8.1 copy-start.67
  689.9 8.1 copy-start.54
  689.9 8.1 copy-start.55
  689.9 28.4 %copy-start.30 = (bf16[4,256,4,64]{1,3,2,0:T(8,128)(2,1)S(1)}, bf16[4,256,4,64]{1,3,2,0:T(8,128)(2,1)}, u32[]{:S(2)}) copy-start(bf16[4,256,4,64]{1,3,2,0:T(8,128)(2,1)} %get-tuple-element.276) | copy-start | bytes 1572868
  693.7 75.7 %all-to-all-start.1 = ((bf16[4,2,65536]{2,1,0:T(2,128)(2,1)}), bf16[4,2,65536]{2,1,0:T(2,128)(2,1)}, u32[]{:S(2)}, u32[]{:S(2)}) async-start(bf16[4,2,65536]{2,1,0:T(2,128)(2,1)} %reshape.433), calls=%async_computation.1 | async-start | bytes 2097152 | tf_op jit(solution)/shard_map/all_to_all | solution.py:227
  697.9 22.7 %copy-start.50 = (bf16[4,256,4,64]{1,3,2,0:T(8,128)(2,1)S(1)}, bf16[4,256,4,64]{1,3,2,0:T(8,128)(2,1)}, u32[]{:S(2)}) copy-start(bf16[4,256,4,64]{1,3,2,0:T(8,128)(2,1)} %get-tuple-element.275) | copy-start | bytes 1572868
  996.9 5.5 copy-start.28
  1002.4 2.5 copy-start.27
  1004.9 2.5 copy-start.34
  1004.9 4.1 copy-start.1
  (41 other events, 57.1 us)
Sparse Core Ops, SparseCore 0:
  9.6 103.7 all-gather.5
  114.9 35.5 all-gather.7
  152.1 58.3 all-gather.9
  211.9 58.2 all-gather.11
  356.8 44.4 reduce-scatter.13
  404.0 71.8 reduce-scatter.17
  478.4 71.7 reduce-scatter.19
  552.9 99.0 reduce-scatter.11
  655.2 20.0 reduce-scatter.21
  677.6 20.0 reduce-scatter.23
  700.2 19.3 reduce-scatter.15
  723.9 272.9 all-reduce.6
where the time goes:
time: 1020 us
  waiting for transfers between devices  527 us (52%)
  matrix products  214 us (21%)
  blocking collectives  103 us (10%)
  other arithmetic  69 us (7%)
  local copies, waits for them, and re-layouts  68.3 us (7%)
  starting transfers between devices  17.2 us (2%)
  between operations  16.8 us (2%)
    psum x1, waiting for transfers between devices, local(): lax.psum(attn_parts[0].astype(jnp.bfloat16), 'rep').astype(jnp.float32)  220 us
    reduce_scatter x1, waiting for transfers between devices, local(): lax.psum_scatter(grad_in_full.astype(jnp.bfloat16), 'shard', scatter_dime...  102 us
    reduce_scatter x1, waiting for transfers between devices, local(): lax.psum_scatter(grad_down.astype(jnp.bfloat16), 'shard', scatter_dimensi...  74.3 us
    dot_general x5, matrix products, matmul(): return jnp.dot(left, right, preferred_element_type=jnp.float32)  51.6 us
    dot_general x10, matrix products, contract_cols(): lax.dot_general(left, right, (((1,), (1,)), ((), ())), preferred_element_...  48.9 us
    all_gather x1, waiting for transfers between devices, local(): lax.all_gather(attn_in, 'shard', axis=1, tiled=True)  44.5 us
    dot_general x10, matrix products, contract_rows(): lax.dot_general(left, right, (((0,), (0,)), ((), ())), preferred_element_...  40.5 us
    psum x1, blocking collectives, local(): lax.psum(attn_parts[2].astype(jnp.bfloat16), 'rep').astype(jnp.float32)  39.4 us
  transfers between devices with their start and end apart: 16, of which 7 were waited for; matrix products, arithmetic and copies ran while one was open for 24% of the time, Pallas kernels for 0%

commit v1 on v0

--- a/solution.py
+++ b/solution.py
@@ -1,6 +1,10 @@
+import types
+
 import jax
 import jax.numpy as jnp
 from jax import lax
+from jax.experimental import pallas as pl
+from jax.experimental.pallas import tpu as pltpu
 from jax.sharding import PartitionSpec as P
 
 HEADS = 16
@@ -152,6 +156,1180 @@
     return (merge_heads(query_grad), merge_heads(key_grad), merge_heads(value_grad))
 
 
+def pick_blocks(blocks, order):
+    count = blocks.shape[0]
+    return jnp.concatenate(
+        [lax.dynamic_slice_in_dim(blocks, order[i], 1, axis=0) for i in range(count)], axis=0
+    )
+
+
+MESH = pl.DeviceIdType.MESH
+ROWS = 128
+CHUNKS = 32
+
+
+def place():
+    rep, shard = lax.axis_index("rep"), lax.axis_index("shard")
+    return rep // 2, lax.rem(rep, 2), shard // 2, lax.rem(shard, 2)
+
+
+def device(z, y, x, c):
+    return (z * 2 + y, x * 2 + c)
+
+
+def greet(peers):
+    barrier = pltpu.get_barrier_semaphore()
+    for peer in peers:
+        pl.semaphore_signal(barrier, inc=1, device_id=peer, device_id_type=MESH)
+    pl.semaphore_wait(barrier, len(peers))
+
+
+def rows_at(base, size, align):
+    return pl.ds(pl.multiple_of(base, align), size)
+
+
+F32, BF16 = jnp.float32, jnp.bfloat16
+RING = 8
+LAGS = (0, 2, 3, 4, 5, 6, 7)
+
+
+def dot_over(left, right, a, b):
+    return lax.dot_general(left, right, (((a,), (b,)), ((), ())), preferred_element_type=F32)
+
+
+def dot_nn(left, right):
+    return dot_over(left, right, 1, 0)
+
+
+def dot_nt(left, right):
+    return dot_over(left, right, 1, 1)
+
+
+def dot_tn(left, right):
+    return dot_over(left, right, 0, 0)
+
+
+def remote(src, dst, send, recv, peer):
+    return pltpu.make_async_remote_copy(
+        src_ref=src, dst_ref=dst, send_sem=send, recv_sem=recv, device_id=peer, device_id_type=MESH
+    )
+
+
+def loop(count, body):
+    def step(i, carry):
+        body(i)
+        return carry
+
+    lax.fori_loop(0, count, step, 0)
+
+
+ERF_TOP = (
+    -2.72614225801306e-10, 2.77068142495902e-08, -2.10102402082508e-06, -5.69250639462346e-05,
+    -7.34990630326855e-04, -2.95459980854025e-03, -1.60960333262415e-02,
+)
+ERF_BOTTOM = (
+    -1.45660718464996e-05, -2.13374055278905e-04, -1.68282697438203e-03, -7.37332916720468e-03,
+    -1.42647390514189e-02,
+)
+
+
+def normal_cdf(value):
+    arg = jnp.clip(value * 0.7071067811865476, -3.832506856900711, 3.832506856900711)
+    square = arg * arg
+    top, bottom = jnp.full_like(arg, ERF_TOP[0]), jnp.full_like(arg, ERF_BOTTOM[0])
+    for factor in ERF_TOP[1:]:
+        top = top * square + factor
+    for factor in ERF_BOTTOM[1:]:
+        bottom = bottom * square + factor
+    return 0.5 + 0.5 * (arg * top / bottom)
+
+
+BACK_SCRATCH = dict(
+    mine=pltpu.VMEM((4, 2, ROWS, 1024), BF16),
+    r0=pltpu.VMEM((RING, 2, ROWS, 1024), BF16),
+    r1=pltpu.VMEM((RING, ROWS, 1024), BF16),
+    r2=pltpu.VMEM((RING, ROWS // 2, 1024), BF16),
+    r3=pltpu.VMEM((RING, 3, ROWS // 8, 1024), BF16),
+    held=pltpu.VMEM((RING, ROWS // 8, 1024), BF16),
+    small=pltpu.VMEM((4, 24, 256), F32),
+    s0=pltpu.VMEM((2, 24, 256), F32),
+    s1=pltpu.VMEM((24, 256), F32),
+    s2=pltpu.VMEM((24, 256), F32),
+    s3=pltpu.VMEM((3, 24, 256), F32),
+    own_sem=pltpu.SemaphoreType.DMA((4, 2)),
+    c_send=pltpu.SemaphoreType.DMA((CHUNKS, 2)),
+    c_recv=pltpu.SemaphoreType.DMA((CHUNKS, 2)),
+    x_send=pltpu.SemaphoreType.DMA((CHUNKS,)),
+    x_recv=pltpu.SemaphoreType.DMA((CHUNKS,)),
+    y_send=pltpu.SemaphoreType.DMA((CHUNKS,)),
+    y_recv=pltpu.SemaphoreType.DMA((CHUNKS,)),
+    z_send=pltpu.SemaphoreType.DMA((CHUNKS, 3)),
+    z_recv=pltpu.SemaphoreType.DMA((CHUNKS, 3)),
+    a_send=pltpu.SemaphoreType.DMA((CHUNKS, 3)),
+    a_recv=pltpu.SemaphoreType.DMA((CHUNKS, 3)),
+    a_own=pltpu.SemaphoreType.DMA((CHUNKS,)),
+    b_send=pltpu.SemaphoreType.DMA((CHUNKS,)),
+    b_recv=pltpu.SemaphoreType.DMA((CHUNKS,)),
+    t_send=pltpu.SemaphoreType.DMA((7,)),
+    t_recv=pltpu.SemaphoreType.DMA((7,)),
+    o_send=pltpu.SemaphoreType.DMA((2, 3)),
+    o_recv=pltpu.SemaphoreType.DMA((2, 3)),
+    o_own=pltpu.SemaphoreType.DMA((2,)),
+    load_sem=pltpu.SemaphoreType.DMA((16,)),
+    tile_sem=pltpu.SemaphoreType.DMA((2, 16)),
+    weight_sem=pltpu.SemaphoreType.DMA((2,)),
+    grad_sem=pltpu.SemaphoreType.DMA((2,)),
+    x1=pltpu.VMEM((512, 1024), BF16),
+    q1=pltpu.VMEM((512, 1024), BF16),
+    k1=pltpu.VMEM((512, 1024), BF16),
+    v1=pltpu.VMEM((512, 1024), BF16),
+    o1=pltpu.VMEM((512, 1024), BF16),
+    h1=pltpu.VMEM((512, 1024), BF16),
+    q2=pltpu.VMEM((512, 1024), BF16),
+    k2=pltpu.VMEM((256, 1024), BF16),
+    v2=pltpu.VMEM((256, 1024), BF16),
+    o2=pltpu.VMEM((512, 1024), BF16),
+    h2=pltpu.VMEM((512, 1024), BF16),
+    e1=pltpu.VMEM((256, 1024), BF16),
+    cot=pltpu.VMEM((512, 1024), BF16),
+    sum1=pltpu.VMEM((512, 1024), F32),
+    sum2=pltpu.VMEM((512, 1024), F32),
+    sum3=pltpu.VMEM((512, 1024), F32),
+    dz=pltpu.VMEM((512, 1024), F32),
+    low=pltpu.VMEM((512, 1024), BF16),
+    dob=pltpu.VMEM((512, 1024), BF16),
+    dqb=pltpu.VMEM((512, 1024), BF16),
+    dkb=pltpu.VMEM((512, 1024), BF16),
+    dvb=pltpu.VMEM((512, 1024), BF16),
+    dka=pltpu.VMEM((512, 128), F32),
+    dva=pltpu.VMEM((512, 128), F32),
+    ut=pltpu.VMEM((2, 512, 512), F32),
+    wd=pltpu.VMEM((2, 512, 1024), BF16),
+    wu=pltpu.VMEM((2, 1024, 512), BF16),
+    wb=pltpu.VMEM((2, 1024, 1024), BF16),
+    gt=pltpu.VMEM((2, 512, 512), BF16),
+    dut=pltpu.VMEM((512, 512), BF16),
+    stage=pltpu.VMEM((2, 4, ROWS, 1024), BF16),
+    sums=pltpu.VMEM((8, 1024), F32),
+    ub=pltpu.VMEM((8, 1, 512), F32),
+)
+BACK_LOADS = (
+    "x1", "q1", "k1", "v1", "o1", "h1", "q2", "k2", "v2", "o2", "h2", "e1", "cot", "sum1", "sum2", "sum3",
+)
+
+
+class Reducer:
+    def __init__(self, s, parts, total, small_total):
+        self.s, self.parts, self.total, self.small_total = s, parts, total, small_total
+        z, y, x, c = self.at = place()
+        self.core = device(z, y, x, 1 - c)
+        self.xmate = device(z, y, 1 - x, c)
+        self.diag = device(z, y, 1 - x, 1 - c)
+        self.ymate = device(z, 1 - y, x, c)
+        self.others = [device(lax.rem(z + i, 4), y, x, c) for i in (1, 2, 3)]
+
+    def greet(self):
+        greet([self.core, self.xmate, self.diag, self.ymate] + self.others)
+
+    def core_copy(self, k, side):
+        s, (_, _, _, c) = self.s, self.at
+        return remote(
+            self.parts.at[k, side * 2 + 1 - c], s.r0.at[lax.rem(k, RING), side],
+            s.c_send.at[k, side], s.c_recv.at[k, side], self.core,
+        )
+
+    def own_copy(self, k, side):
+        s, (_, _, _, c) = self.s, self.at
+        slot = lax.rem(k, 4)
+        return pltpu.make_async_copy(
+            self.parts.at[k, side * 2 + c], s.mine.at[slot, side], s.own_sem.at[slot, side]
+        )
+
+    def fetch(self, k):
+        for side in (0, 1):
+            self.core_copy(k, side).start()
+            self.own_copy(k, side).start()
+
+    def x_copy(self, k):
+        s, (_, _, x, _) = self.s, self.at
+        slot = lax.rem(k, RING)
+        return remote(s.r0.at[slot, 1 - x], s.r1.at[slot], s.x_send.at[k], s.x_recv.at[k], self.xmate)
+
+    def core_sum(self, k):
+        s, slot, near = self.s, lax.rem(k, RING), lax.rem(k, 4)
+        for side in (0, 1):
+            self.core_copy(k, side).wait()
+            self.own_copy(k, side).wait()
+
+        def add(i):
+            piece = rows_at(i * 32, 32, 32)
+            for side in (0, 1):
+                s.r0[slot, side, piece, :] = s.r0[slot, side, piece, :] + s.mine[near, side, piece, :]
+
+        loop(ROWS // 32, add)
+        self.x_copy(k).start()
+
+    def y_copy(self, k):
+        s, (_, y, _, _) = self.s, self.at
+        slot, half = lax.rem(k, RING), ROWS // 2
+        return remote(
+            s.r1.at[slot, rows_at((1 - y) * half, half, half), :], s.r2.at[slot],
+            s.y_send.at[k], s.y_recv.at[k], self.ymate,
+        )
+
+    def x_sum(self, k):
+        s, (_, _, x, _) = self.s, self.at
+        slot = lax.rem(k, RING)
+        self.x_copy(k).wait()
+
+        def add(i):
+            piece = rows_at(i * 32, 32, 32)
+            s.r1[slot, piece, :] = s.r0[slot, x, piece, :] + s.r1[slot, piece, :]
+
+        loop(ROWS // 32, add)
+        self.y_copy(k).start()
+
+    def z_copies(self, k):
+        s, (z, _, _, _) = self.s, self.at
+        slot, quarter = lax.rem(k, RING), ROWS // 8
+        return [
+            remote(
+                s.r2.at[slot, rows_at(lax.rem(z + i + 1, 4) * quarter, quarter, quarter), :], s.r3.at[slot, i],
+                s.z_send.at[k, i], s.z_recv.at[k, i], self.others[i],
+            )
+            for i in (0, 1, 2)
+        ]
+
+    def y_sum(self, k):
+        s, (_, y, _, _) = self.s, self.at
+        slot, half = lax.rem(k, RING), ROWS // 2
+        self.y_copy(k).wait()
+
+        def add(i):
+            piece = rows_at(i * 32, 32, 32)
+            s.r2[slot, piece, :] = s.r1[slot, rows_at(y * half + i * 32, 32, 32), :] + s.r2[slot, piece, :]
+
+        loop(half // 32, add)
+        for copy in self.z_copies(k):
+            copy.start()
+
+    def out_piece(self, k):
+        z, y, _, _ = self.at
+        return self.total.at[k, rows_at(y * (ROWS // 2) + z * (ROWS // 8), ROWS // 8, ROWS // 8), :]
+
+    def spread_copies(self, k):
+        s, slot = self.s, lax.rem(k, RING)
+        return [
+            remote(s.held.at[slot], self.out_piece(k), s.a_send.at[k, i], s.a_recv.at[k, i], self.others[i])
+            for i in (0, 1, 2)
+        ]
+
+    def held_copy(self, k):
+        return pltpu.make_async_copy(self.s.held.at[lax.rem(k, RING)], self.out_piece(k), self.s.a_own.at[k])
+
+    def z_sum(self, k):
+        s, (z, _, _, _) = self.s, self.at
+        slot, quarter = lax.rem(k, RING), ROWS // 8
+        for copy in self.z_copies(k):
+            copy.wait()
+        added = s.r2[slot, rows_at(z * quarter, quarter, quarter), :].astype(F32)
+        for i in (0, 1, 2):
+            added = added + s.r3[slot, i].astype(F32)
+        s.held[slot] = added.astype(BF16)
+        for copy in self.spread_copies(k):
+            copy.start()
+        self.held_copy(k).start()
+
+    def half_copy(self, k):
+        s, (_, y, _, _) = self.s, self.at
+        half = ROWS // 2
+        part = self.total.at[k, rows_at(y * half, half, half), :]
+        return remote(part, part, s.b_send.at[k], s.b_recv.at[k], self.ymate)
+
+    def spread_y(self, k):
+        for copy in self.spread_copies(k):
+            copy.wait()
+        self.held_copy(k).wait()
+        self.half_copy(k).start()
+
+    def finish(self, k):
+        self.half_copy(k).wait()
+
+    def tick(self, t):
+        stages = (self.fetch, self.core_sum, self.x_sum, self.y_sum, self.z_sum, self.spread_y, self.finish)
+        for lag, act in zip(LAGS, stages):
+            k = t - lag
+
+            @pl.when((k >= 0) & (k < CHUNKS))
+            def _(k=k, act=act):
+                act(k)
+
+    def small_steps(self, t):
+        s, (_, _, x, c) = self.s, self.at
+        send, recv = s.t_send, s.t_recv
+        firsts = [
+            remote(s.small.at[side * 2 + 1 - c], s.s0.at[side], send.at[side], recv.at[side], self.core)
+            for side in (0, 1)
+        ]
+        across = remote(s.s0.at[1 - x], s.s1, send.at[2], recv.at[2], self.xmate)
+        along = remote(s.s1, s.s2, send.at[3], recv.at[3], self.ymate)
+        lasts = [
+            remote(s.s2, s.s3.at[i], send.at[4 + i], recv.at[4 + i], self.others[i]) for i in (0, 1, 2)
+        ]
+
+        @pl.when(t == 0)
+        def _():
+            for copy in firsts:
+                copy.start()
+
+        @pl.when(t == 2)
+        def _():
+            for side in (0, 1):
+                firsts[side].wait()
+                s.s0[side] = s.s0[side] + s.small[side * 2 + c]
+            across.start()
+
+        @pl.when(t == 4)
+        def _():
+            across.wait()
+            s.s1[...] = s.s1[...] + s.s0[x]
+            along.start()
+
+        @pl.when(t == 6)
+        def _():
+            along.wait()
+            s.s2[...] = s.s2[...] + s.s1[...]
+            for copy in lasts:
+                copy.start()
+
+        @pl.when(t == 8)
+        def _():
+            for copy in lasts:
+                copy.wait()
+            self.small_total[...] = s.s2[...] + s.s3[0] + s.s3[1] + s.s3[2]
+
+
+def back_kernel(*refs):
+    loads = dict(zip(BACK_LOADS, refs[:16]))
+    d_all, g_all, f_in, f_out, f_up, f_down, gains, out_rows, mask = refs[16:25]
+    total, small_total, grad_enc, out_back, grad_back, parts = refs[25:31]
+    s = types.SimpleNamespace(**dict(zip(BACK_SCRATCH, refs[31:])))
+    reducer = Reducer(s, parts, total, small_total)
+    z, y, x, c = reducer.at
+    mine = x * 2 + c
+    peers = ((reducer.core, x * 2 + 1 - c), (reducer.xmate, (1 - x) * 2 + c), (reducer.diag, (1 - x) * 2 + 1 - c))
+
+    def row_copies(which, src, dst):
+        return [
+            remote(
+                src.at[rows_at(slot * 128, 128, 128), :], dst.at[mine],
+                s.o_send.at[which, i], s.o_recv.at[which, i], peer,
+            )
+            for i, (peer, slot) in enumerate(peers)
+        ] + [pltpu.make_async_copy(src.at[rows_at(mine * 128, 128, 128), :], dst.at[mine], s.o_own.at[which])]
+
+    def load(name):
+        return pltpu.make_async_copy(loads[name], getattr(s, name), s.load_sem.at[BACK_LOADS.index(name)])
+
+    for name in ("sum3", "cot", "h2"):
+        load(name).start()
+
+    def tile_copies(j, slot):
+        copies = []
+        for i in range(4):
+            columns = rows_at(i * 1024 + j * 128, 128, 128)
+            copies += [
+                pltpu.make_async_copy(
+                    d_all.at[:, columns], s.ut.at[slot, :, pl.ds(i * 128, 128)], s.tile_sem.at[slot, i]
+                ),
+                pltpu.make_async_copy(
+                    g_all.at[:, columns], s.gt.at[slot, :, pl.ds(i * 128, 128)], s.tile_sem.at[slot, 12 + i]
+                ),
+                pltpu.make_async_copy(
+                    f_down.at[columns, :], s.wd.at[slot, pl.ds(i * 128, 128), :], s.tile_sem.at[slot, 4 + i]
+                ),
+                pltpu.make_async_copy(
+                    f_up.at[:, columns], s.wu.at[slot, :, pl.ds(i * 128, 128)], s.tile_sem.at[slot, 8 + i]
+                ),
+            ]
+        return copies
+
+    for copy in tile_copies(0, 0):
+        copy.start()
+    weights = (
+        f_out.at[1], f_in.at[4], f_in.at[5], f_in.at[3], f_out.at[0], f_in.at[0], f_in.at[1], f_in.at[2],
+    )
+
+    def weight(i):
+        return pltpu.make_async_copy(weights[i], s.wb.at[i % 2], s.weight_sem.at[i % 2])
+
+    reducer.greet()
+    for copy in row_copies(0, out_rows, out_back):
+        copy.start()
+    for name in ("sum2", "o2", "q2", "k2", "v2", "h1", "e1", "sum1", "o1", "q1", "k1", "v1", "x1"):
+        load(name).start()
+    weight(0).start()
+    weight(1).start()
+    s.small[...] = jnp.zeros_like(s.small)
+
+    def put(row, value):
+        for i in range(4):
+            s.small[i, row:row + 1, :] = value[:, i * 256:(i + 1) * 256]
+
+    def norm_back(sum_ref, index, first, bias_row):
+        s.sums[...] = jnp.zeros_like(s.sums)
+        gain = gains[6 + index:7 + index, :]
+
+        def block(i):
+            p = rows_at(i * 32, 32, 32)
+            value = sum_ref[p, :]
+            grad = s.cot[p, :].astype(F32) * mask[p, 0:1] if first else s.dz[p, :]
+            center = value - jnp.mean(value, axis=1, keepdims=True)
+            scale = lax.rsqrt(jnp.mean(center * center, axis=1, keepdims=True) + epsilon)
+            normal = center * scale
+            scaled = grad * gain
+            back = scale * (
+                scaled - jnp.mean(scaled, axis=1, keepdims=True)
+                - normal * jnp.mean(scaled * normal, axis=1, keepdims=True)
+            )
+            rounded = back.astype(BF16)
+            s.dz[p, :] = back
+            s.low[p, :] = rounded
+            s.sums[0:1, :] += jnp.sum(grad * normal, axis=0, keepdims=True)
+            s.sums[1:2, :] += jnp.sum(grad, axis=0, keepdims=True)
+            s.sums[2:3, :] += jnp.sum(rounded.astype(F32), axis=0, keepdims=True)
+
+        loop(16, block)
+        put(6 + index, s.sums[0:1, :])
+        put(9 + index, s.sums[1:2, :])
+        put(bias_row, s.sums[2:3, :])
+
+    def column_sums(ref, count, row):
+        s.sums[...] = jnp.zeros_like(s.sums)
+
+        def block(i):
+            p = rows_at(i * 64, 64, 64)
+            s.sums[0:1, :] += jnp.sum(ref[p, :].astype(F32), axis=0, keepdims=True)
+
+        loop(count // 64, block)
+        put(row, s.sums[0:1, :])
+
+    pending = []
+
+    def flush():
+        if pending:
+            pending.pop().wait()
+
+    def store_grad(chunk, left, right):
+        count = left.shape[0]
+        flush()
+
+        def block(i):
+            product = dot_tn(left[:, rows_at(i * 256, 256, 256)], right[0:count, :]).astype(BF16)
+            s.stage[0, i] = product[:128]
+            s.stage[1, i] = product[128:]
+
+        loop(4, block)
+        pending.append(pltpu.make_async_copy(s.stage, parts.at[pl.ds(chunk, 2)], s.grad_sem.at[0]))
+        pending[-1].start()
+
+    load("sum3").wait()
+    load("cot").wait()
+    norm_back(s.sum3, 2, True, 16)
+    load("h2").wait()
+
+    def down_save(j):
+        return pltpu.make_async_copy(s.stage.at[0], parts.at[2 * j], s.grad_sem.at[0])
+
+    def up_save(j):
+        return pltpu.make_async_copy(s.stage.at[1], parts.at[2 * j + 1], s.grad_sem.at[1])
+
+    def tile(j):
+        slot = lax.rem(j, 2)
+        for copy in tile_copies(j, slot):
+            copy.wait()
+
+        @pl.when(j < 7)
+        def _():
+            for copy in tile_copies(j + 1, 1 - slot):
+                copy.start()
+
+        def hidden(i):
+            p = rows_at(i * 256, 256, 256)
+            grad = dot_nt(s.low[...], s.wd[slot, p, :])
+            rounded = (grad * s.ut[slot, :, p]).astype(BF16)
+            s.dut[:, p] = rounded
+            s.ub[j, :, p] = jnp.sum(rounded.astype(F32), axis=0, keepdims=True)
+
+        loop(2, hidden)
+
+        def down(i):
+            product = dot_tn(s.gt[slot, :, rows_at(i * 256, 256, 256)], s.low[...]).astype(BF16)
+            s.stage[0, 2 * i] = product[:128]
+            s.stage[0, 2 * i + 1] = product[128:]
+
+        loop(2, down)
+        down_save(j).start()
+
+        def up(i):
+            product = dot_tn(s.h2[:, rows_at(i * 256, 256, 256)], s.dut[...]).astype(BF16)
+            s.stage[1, i, :, 0:512] = product[:128]
+            s.stage[1, i, :, 512:1024] = product[128:]
+
+        loop(4, up)
+        up_save(j).start()
+
+        def back(i):
+            p = rows_at(i * 256, 256, 256)
+            s.dz[:, p] += dot_nt(s.dut[...], s.wu[slot, p, :])
+
+        loop(4, back)
+        down_save(j).wait()
+        up_save(j).wait()
+        loop(2 - lax.rem(j, 2), lambda i: reducer.tick((3 * j + 1) // 2 + i))
+
+    loop(8, tile)
+    for j in range(8):
+        for i in range(4):
+            s.small[i, 12 + j // 2:13 + j // 2, (j % 2) * 128:(j % 2) * 128 + 128] = s.ub[j, :, i * 128:(i + 1) * 128]
+    load("sum2").wait()
+    norm_back(s.sum2, 1, False, 5)
+    reducer.tick(12)
+    load("o2").wait()
+    store_grad(16, s.o2, s.low)
+
+    def times_weight(dst, left, count, slot):
+        def block(i):
+            p = rows_at(i * 256, 256, 256)
+            dst[:, p] = dot_nt(left[...], s.wb[slot, p, :]).astype(BF16)
+
+        loop(count, block)
+
+    def add_weight(left, slot):
+        def block(i):
+            p = rows_at(i * 256, 256, 256)
+            s.dz[:, p] += dot_nt(left[...], s.wb[slot, p, :])
+
+        loop(4, block)
+
+    weight(0).wait()
+    times_weight(s.dob, s.low, 4, 0)
+    weight(2).start()
+    flush()
+    reducer.tick(13)
+    for name in ("q2", "k2", "v2"):
+        load(name).wait()
+
+    lane = lax.broadcasted_iota(jnp.int32, (1, 128), 1)
+    head_masks = [(lane < 64).astype(F32).astype(BF16), (lane >= 64).astype(F32).astype(BF16)]
+
+    def attention_pair(i, q_ref, k_ref, v_ref, key_count, causal):
+        lanes = rows_at(i * 128, 128, 128)
+        s.dka[...] = jnp.zeros_like(s.dka)
+        s.dva[...] = jnp.zeros_like(s.dva)
+        for block in (0, 1):
+            rows = pl.ds(block * 256, 256)
+            reach = (block + 1) * 256 if causal else key_count
+            query, grad = q_ref[rows, lanes], s.dob[rows, lanes]
+            key, value = k_ref[0:reach, lanes], v_ref[0:reach, lanes]
+            query_grad = jnp.zeros((256, 128), F32)
+            for mask in head_masks:
+                query_one, grad_one = query * mask, grad * mask
+                scores = dot_nt(key, query_one) * 0.125
+                if causal:
+                    key_at = lax.broadcasted_iota(jnp.int32, (reach, 256), 0)
+                    query_at = lax.broadcasted_iota(jnp.int32, (reach, 256), 1) + block * 256
+                    scores = jnp.where(key_at <= query_at, scores, -1e30)
+                peak = jnp.max(scores, axis=0, keepdims=True)
+                full = jnp.exp(scores - peak)
+                full = full * (1.0 / jnp.sum(full, axis=0, keepdims=True))
+                full_grad = dot_nt(value, grad_one)
+                row_dot = jnp.sum(full * full_grad, axis=0, keepdims=True)
+                score_grad = (full * (full_grad - row_dot)).astype(BF16)
+                s.dva[0:reach, :] += dot_nn(full.astype(BF16), grad_one)
+                s.dka[0:reach, :] += dot_nn(score_grad, query_one)
+                query_grad = query_grad + dot_tn(score_grad, key * mask)
+            s.dqb[rows, lanes] = (query_grad * 0.125).astype(BF16)
+        s.dkb[0:key_count, lanes] = (s.dka[0:key_count, :] * 0.125).astype(BF16)
+        s.dvb[0:key_count, lanes] = s.dva[0:key_count, :].astype(BF16)
+
+    def cross(i):
+        attention_pair(i, s.q2, s.k2, s.v2, 256, False)
+
+        @pl.when((lax.rem(i, 2) == 1) & (i < 7))
+        def _():
+            reducer.tick(14 + i // 2)
+
+    loop(8, cross)
+    load("h1").wait()
+    load("e1").wait()
+    store_grad(18, s.h1, s.dqb)
+    reducer.tick(17)
+    store_grad(20, s.e1, s.dkb)
+    reducer.tick(18)
+    store_grad(22, s.e1, s.dvb)
+    reducer.tick(19)
+    column_sums(s.dqb, 512, 3)
+    column_sums(s.dvb, 256, 4)
+    weight(1).wait()
+    weight(2).wait()
+
+    def enc_block(i):
+        p = rows_at(i * 256, 256, 256)
+        grad_enc[:, p] = (
+            dot_nt(s.dkb[0:256, :], s.wb[1, p, :]) + dot_nt(s.dvb[0:256, :], s.wb[0, p, :])
+        ).astype(BF16)
+
+    loop(4, enc_block)
+    flush()
+    reducer.tick(20)
+    weight(3).start()
+    weight(4).start()
+    weight(3).wait()
+    add_weight(s.dqb, 1)
+    weight(5).start()
+    reducer.tick(21)
+    load("sum1").wait()
+    norm_back(s.sum1, 0, False, 2)
+    load("o1").wait()
+    store_grad(24, s.o1, s.low)
+    reducer.tick(22)
+    weight(4).wait()
+    times_weight(s.dob, s.low, 4, 0)
+    weight(6).start()
+    flush()
+    reducer.tick(23)
+    for name in ("q1", "k1", "v1"):
+        load(name).wait()
+
+    def own(i):
+        attention_pair(i, s.q1, s.k1, s.v1, 512, True)
+
+        @pl.when(lax.rem(i, 3) == 2)
+        def _():
+            reducer.tick(24 + i // 3)
+
+    loop(8, own)
+    load("x1").wait()
+    store_grad(26, s.x1, s.dqb)
+    store_grad(28, s.x1, s.dkb)
+    reducer.tick(26)
+    store_grad(30, s.x1, s.dvb)
+    reducer.tick(27)
+    column_sums(s.dqb, 512, 0)
+    column_sums(s.dvb, 512, 1)
+    flush()
+    reducer.tick(28)
+    weight(5).wait()
+    add_weight(s.dqb, 1)
+    weight(7).start()
+    reducer.tick(29)
+    weight(6).wait()
+    add_weight(s.dkb, 0)
+    reducer.tick(30)
+    weight(7).wait()
+
+    def last(i):
+        p = rows_at(i * 256, 256, 256)
+        s.low[:, p] = (s.dz[:, p] + dot_nt(s.dvb[...], s.wb[1, p, :])).astype(BF16)
+
+    loop(4, last)
+    for copy in row_copies(1, s.low, grad_back):
+        copy.start()
+
+    def drain(i):
+        reducer.tick(31 + i)
+        reducer.small_steps(i)
+
+    loop(max(9, CHUNKS + LAGS[-1] - 31), drain)
+    for copy in row_copies(0, out_rows, out_back) + row_copies(1, s.low, grad_back):
+        copy.wait()
+
+
+def backward(loads, *rest):
+    any_space = pl.BlockSpec(memory_space=pl.ANY)
+    in_vmem = pl.BlockSpec(memory_space=pltpu.VMEM)
+    return pl.pallas_call(
+        back_kernel,
+        out_shape=(
+            jax.ShapeDtypeStruct((CHUNKS, ROWS, 1024), BF16),
+            jax.ShapeDtypeStruct((24, 256), F32),
+            jax.ShapeDtypeStruct((256, 1024), BF16),
+            jax.ShapeDtypeStruct((4, 128, 1024), BF16),
+            jax.ShapeDtypeStruct((4, 128, 1024), BF16),
+            jax.ShapeDtypeStruct((CHUNKS, 4, ROWS, 1024), BF16),
+        ),
+        in_specs=[any_space] * 22 + [in_vmem] * 3,
+        out_specs=(any_space, in_vmem, in_vmem, any_space, any_space, any_space),
+        scratch_shapes=list(BACK_SCRATCH.values()),
+        compiler_params=pltpu.CompilerParams(
+            collective_id=1, has_side_effects=True, vmem_limit_bytes=62 << 20
+        ),
+    )(*[loads[name] for name in BACK_LOADS], *rest)
+
+
+FORWARD_SCRATCH = dict(
+    v_in=pltpu.VMEM((6, 1024, 1024), BF16),
+    v_out=pltpu.VMEM((2, 1024, 1024), BF16),
+    v_up=pltpu.VMEM((1024, 4096), BF16),
+    v_down=pltpu.VMEM((4096, 1024), BF16),
+    v_small=pltpu.VMEM((4, 24, 256), F32),
+    vec=pltpu.VMEM((24, 1024), F32),
+    x=pltpu.VMEM((512, 1024), BF16),
+    e=pltpu.VMEM((256, 1024), BF16),
+    q=pltpu.VMEM((512, 1024), BF16),
+    k=pltpu.VMEM((512, 1024), BF16),
+    v=pltpu.VMEM((512, 1024), BF16),
+    o=pltpu.VMEM((512, 1024), BF16),
+    h1=pltpu.VMEM((512, 1024), BF16),
+    q2=pltpu.VMEM((512, 1024), BF16),
+    k2=pltpu.VMEM((256, 1024), BF16),
+    v2=pltpu.VMEM((256, 1024), BF16),
+    o2=pltpu.VMEM((512, 1024), BF16),
+    h2=pltpu.VMEM((512, 1024), BF16),
+    y=pltpu.VMEM((512, 1024), BF16),
+    hf=pltpu.VMEM((512, 1024), F32),
+    sum_a=pltpu.VMEM((512, 1024), F32),
+    sum_b=pltpu.VMEM((512, 1024), F32),
+    ublock=pltpu.VMEM((512, 256), F32),
+    gblock=pltpu.VMEM((2, 512, 256), BF16),
+    dblock=pltpu.VMEM((2, 512, 256), F32),
+    own_sem=pltpu.SemaphoreType.DMA((16,)),
+    x_send=pltpu.SemaphoreType.DMA((16,)),
+    x_recv=pltpu.SemaphoreType.DMA((16,)),
+    y_send=pltpu.SemaphoreType.DMA((16, 2)),
+    y_recv=pltpu.SemaphoreType.DMA((16, 2)),
+    z_send=pltpu.SemaphoreType.DMA((16, 2)),
+    z_recv=pltpu.SemaphoreType.DMA((16, 2)),
+    c_send=pltpu.SemaphoreType.DMA((16, 2)),
+    c_recv=pltpu.SemaphoreType.DMA((16, 2)),
+    t_send=pltpu.SemaphoreType.DMA((3, 3)),
+    t_recv=pltpu.SemaphoreType.DMA((3, 3)),
+    t_own=pltpu.SemaphoreType.DMA((4,)),
+    save_sem=pltpu.SemaphoreType.DMA((16,)),
+    weight_sem=pltpu.SemaphoreType.DMA((16,)),
+    block_sem=pltpu.SemaphoreType.DMA((2, 2)),
+)
+SAVED = ("x", "q", "k", "v", "o", "h1", "q2", "k2", "v2", "o2", "h2", "sum1", "sum2", "sum3", "y")
+GATHER_ORDER = (0, 1, 2, 6, 4, 5, 3, 7, 8, 9, 10, 11, 12, 13, 14, 15)
+
+
+def weight_rows(refs, k, shard, start, size):
+    if k < 6:
+        return refs[0].at[k, rows_at(shard * 256 + start, size, 8), :]
+    if k < 8:
+        return refs[1].at[k - 6, rows_at(shard * 256 + start, size, 8), :]
+    if k < 12:
+        return refs[2].at[rows_at(shard * 256 + (k - 8) * 64 + start, size, 8), :]
+    return refs[3].at[rows_at(shard * 1024 + (k - 12) * 256 + start, size, 8), :]
+
+
+class Gatherer:
+    def __init__(self, s, shards, full):
+        self.s, self.shards, self.full, self.done = s, shards, full, -4
+        z, y, x, c = self.at = place()
+        self.side = lax.rem(z, 2)
+        self.core = device(z, y, x, 1 - c)
+        self.xmate = device(z, y, 1 - x, c)
+        self.diag = device(z, y, 1 - x, 1 - c)
+        self.ymate = device(z, 1 - y, x, c)
+        self.zmate = device(z + 1 - 2 * self.side, y, x, c)
+        self.mine, self.other = x * 2 + c, (1 - x) * 2 + c
+
+    def greet(self):
+        greet([self.core, self.xmate, self.diag, self.ymate, self.zmate])
+
+    def size(self, k):
+        return 64 if 8 <= k < 12 else 256
+
+    def x_copy(self, k):
+        n = self.size(k) // 4
+        q = (self.at[1] * 2 + self.side) * n
+        return remote(
+            weight_rows(self.shards, k, 0, q, n), weight_rows(self.full, k, self.mine, q, n),
+            self.s.x_send.at[k], self.s.x_recv.at[k], self.xmate,
+        )
+
+    def core_copy(self, k):
+        return remote(
+            weight_rows(self.shards, k, 0, 0, self.size(k)), weight_rows(self.full, k, self.mine, 0, self.size(k)),
+            self.s.c_send.at[k, 0], self.s.c_recv.at[k, 0], self.core,
+        )
+
+    def own_copy(self, k):
+        return pltpu.make_async_copy(
+            weight_rows(self.shards, k, 0, 0, self.size(k)), weight_rows(self.full, k, self.mine, 0, self.size(k)),
+            self.s.own_sem.at[k],
+        )
+
+    def relay(self, k, start, n, send, recv, peer):
+        view = weight_rows(self.full, k, self.other, start, n)
+        return remote(view, view, send, recv, peer)
+
+    def first_hops(self, k):
+        s, n = self.s, self.size(k) // 4
+        q = (self.at[1] * 2 + self.side) * n
+        return [
+            self.relay(k, q, n, s.y_send.at[k, 0], s.y_recv.at[k, 0], self.ymate),
+            self.relay(k, q, n, s.z_send.at[k, 0], s.z_recv.at[k, 0], self.zmate),
+        ]
+
+    def second_hops(self, k):
+        s, n, y = self.s, self.size(k) // 4, self.at[1]
+        return [
+            self.relay(k, (y * 2 + 1 - self.side) * n, n // 2, s.y_send.at[k, 1], s.y_recv.at[k, 1], self.ymate),
+            self.relay(
+                k, ((1 - y) * 2 + self.side) * n + n // 2, n // 2, s.z_send.at[k, 1], s.z_recv.at[k, 1], self.zmate
+            ),
+        ]
+
+    def last_hop(self, k):
+        return self.relay(k, 0, self.size(k), self.s.c_send.at[k, 1], self.s.c_recv.at[k, 1], self.core)
+
+    def step(self, t):
+        def chunk(lag):
+            return GATHER_ORDER[t - lag] if 0 <= t - lag < 16 else None
+
+        if (k := chunk(-3)) is not None:
+            self.x_copy(k).start()
+            self.core_copy(k).start()
+            self.own_copy(k).start()
+        if (k := chunk(0)) is not None:
+            self.x_copy(k).wait()
+            for copy in self.first_hops(k):
+                copy.start()
+        if (k := chunk(1)) is not None:
+            for copy in self.first_hops(k):
+                copy.wait()
+            for copy in self.second_hops(k):
+                copy.start()
+        if (k := chunk(2)) is not None:
+            for copy in self.second_hops(k):
+                copy.wait()
+            self.last_hop(k).start()
+        if (k := chunk(3)) is not None:
+            self.last_hop(k).wait()
+            self.core_copy(k).wait()
+            self.own_copy(k).wait()
+
+    def advance(self, t):
+        while self.done < t:
+            self.done += 1
+            self.step(self.done)
+
+    def ready(self, index):
+        self.advance(index + 3)
+
+
+def forward_kernel(*refs):
+    w_in, w_out, w_up, w_down, small, tok, cot, enc, mask = refs[:9]
+    f_in, f_out, f_up, f_down, f_cot, gains, g_all, d_all = refs[9:17]
+    saved = dict(zip(SAVED, refs[17:32]))
+    s = types.SimpleNamespace(**dict(zip(FORWARD_SCRATCH, refs[32:])))
+    full = (s.v_in, s.v_out, s.v_up, s.v_down)
+    gather = Gatherer(s, (w_in, w_out, w_up, w_down), full)
+    mine, (_, _, x, c) = gather.mine, gather.at
+    peers = ((gather.core, x * 2 + 1 - c), (gather.xmate, gather.other), (gather.diag, (1 - x) * 2 + 1 - c))
+
+    def rows_of(index):
+        return rows_at(index * 128, 128, 128)
+
+    def token_copies():
+        return [
+            remote(tok.at[slot], s.x.at[rows_of(mine), :], s.t_send.at[0, i], s.t_recv.at[0, i], peer)
+            for i, (peer, slot) in enumerate(peers)
+        ] + [
+            remote(small, s.v_small.at[mine], s.t_send.at[2, i], s.t_recv.at[2, i], peer)
+            for i, (peer, slot) in enumerate(peers)
+        ] + [
+            pltpu.make_async_copy(tok.at[mine], s.x.at[rows_of(mine), :], s.t_own.at[0]),
+            pltpu.make_async_copy(small, s.v_small.at[mine], s.t_own.at[1]),
+        ]
+
+    def cot_copies():
+        return [
+            remote(cot.at[slot], f_cot.at[mine], s.t_send.at[1, i], s.t_recv.at[1, i], peer)
+            for i, (peer, slot) in enumerate(peers)
+        ] + [pltpu.make_async_copy(cot.at[mine], f_cot.at[mine], s.t_own.at[2])]
+
+    enc_copy = pltpu.make_async_copy(enc, s.e, s.t_own.at[3])
+    gather.greet()
+    enc_copy.start()
+    gather.advance(-2)
+    for copy in token_copies():
+        copy.start()
+
+    def save(name, ref):
+        return pltpu.make_async_copy(ref, saved[name], s.save_sem.at[SAVED.index(name)])
+
+    def weight_saves(k):
+        if k < 6:
+            return [pltpu.make_async_copy(s.v_in.at[k], f_in.at[k], s.weight_sem.at[k])]
+        if k < 8:
+            return [pltpu.make_async_copy(s.v_out.at[k - 6], f_out.at[k - 6], s.weight_sem.at[k])]
+        if k == 11:
+            return [pltpu.make_async_copy(s.v_up, f_up, s.weight_sem.at[k])]
+        if k == 15:
+            return [pltpu.make_async_copy(s.v_down, f_down, s.weight_sem.at[k])]
+        return []
+
+    def ready(index):
+        gather.ready(index)
+        for copy in weight_saves(GATHER_ORDER[index]):
+            copy.start()
+
+    def project(dst, left, weight, count, bias):
+        def block(i):
+            columns = rows_at(i * 256, 256, 256)
+            product = dot_nn(left[0:count, :], weight[:, columns])
+            if bias is not None:
+                product = product + s.vec[bias:bias + 1, columns]
+            dst[0:count, columns] = product.astype(BF16)
+
+        loop(4, block)
+
+    def join(dst, base, left, weight, bias):
+        def block(i):
+            columns = rows_at(i * 256, 256, 256)
+            dst[:, columns] = base[:, columns].astype(F32) + (
+                dot_nn(left[...], weight[:, columns]) + s.vec[bias:bias + 1, columns]
+            )
+
+        loop(4, block)
+
+    def normalize(sum_ref, index, low, last):
+        gain, shift = s.vec[6 + index:7 + index, :], s.vec[9 + index:10 + index, :]
+
+        def block(i):
+            p = rows_at(i * 32, 32, 32)
+            value = sum_ref[p, :]
+            center = value - jnp.mean(value, axis=1, keepdims=True)
+            scale = lax.rsqrt(jnp.mean(center * center, axis=1, keepdims=True) + epsilon)
+            result = center * scale * gain + shift
+            if last:
+                low[p, :] = (result * mask[p, 0:1]).astype(BF16)
+            else:
+                s.hf[p, :] = result
+                low[p, :] = result.astype(BF16)
+
+        loop(16, block)
+
+    lane = lax.broadcasted_iota(jnp.int32, (1, 128), 1)
+    head_masks = [(lane < 64).astype(F32).astype(BF16), (lane >= 64).astype(F32).astype(BF16)]
+
+    def attend_pair(i, q_ref, k_ref, v_ref, o_ref, key_count, causal):
+        lanes = rows_at(i * 128, 128, 128)
+        for block in (0, 1):
+            rows = pl.ds(block * 256, 256)
+            reach = (block + 1) * 256 if causal else key_count
+            query = q_ref[rows, lanes]
+            key, value = k_ref[0:reach, lanes], v_ref[0:reach, lanes]
+            context = jnp.zeros((256, 128), F32)
+            for head_mask in head_masks:
+                scores = dot_nt(query * head_mask, key) * 0.125
+                if causal:
+                    query_at = lax.broadcasted_iota(jnp.int32, (256, reach), 0) + block * 256
+                    key_at = lax.broadcasted_iota(jnp.int32, (256, reach), 1)
+                    scores = jnp.where(key_at <= query_at, scores, -1e30)
+                weights = jnp.exp(scores - jnp.max(scores, axis=1, keepdims=True))
+                weights = weights * (1.0 / jnp.sum(weights, axis=1, keepdims=True))
+                context = context + dot_nn(weights.astype(BF16), value * head_mask)
+            o_ref[rows, lanes] = context.astype(BF16)
+
+    ready(0)
+    for copy in token_copies():
+        copy.wait()
+    for i in range(4):
+        s.vec[:, i * 256:(i + 1) * 256] = s.v_small[i]
+    gains[...] = s.vec[0:16, :]
+    save("x", s.x).start()
+    project(s.q, s.x, s.v_in.at[0], 512, 0)
+    save("q", s.q).start()
+    ready(1)
+    project(s.k, s.x, s.v_in.at[1], 512, None)
+    save("k", s.k).start()
+    ready(2)
+    project(s.v, s.x, s.v_in.at[2], 512, 1)
+    save("v", s.v).start()
+    for part in range(4):
+        loop(2, lambda i, part=part: attend_pair(part * 2 + i, s.q, s.k, s.v, s.o, 512, True))
+        gather.advance(6 + part)
+    save("o", s.o).start()
+    ready(3)
+    join(s.sum_a, s.x, s.o, s.v_out.at[0], 2)
+    save("sum1", s.sum_a).start()
+    ready(4)
+    normalize(s.sum_a, 0, s.h1, False)
+    save("h1", s.h1).start()
+    enc_copy.wait()
+    project(s.k2, s.e, s.v_in.at[4], 256, None)
+    save("k2", s.k2).start()
+    ready(5)
+    project(s.v2, s.e, s.v_in.at[5], 256, 4)
+    save("v2", s.v2).start()
+    ready(6)
+    project(s.q2, s.h1, s.v_in.at[3], 512, 3)
+    save("q2", s.q2).start()
+    ready(7)
+    for part in range(4):
+        loop(2, lambda i, part=part: attend_pair(part * 2 + i, s.q2, s.k2, s.v2, s.o2, 256, False))
+        gather.advance(11 + part // 2)
+    save("o2", s.o2).start()
+    join(s.sum_b, s.hf, s.o2, s.v_out.at[1], 5)
+    save("sum2", s.sum_b).start()
+    ready(10)
+    normalize(s.sum_b, 1, s.h2, False)
+    save("h2", s.h2).start()
+    for copy in cot_copies():
+        copy.start()
+    save("sum1", s.sum_a).wait()
+
+    def widen(i):
+        p = rows_at(i * 64, 64, 64)
+        s.sum_a[p, :] = s.hf[p, :] + s.vec[16:17, :]
+
+    loop(8, widen)
+    ready(11)
+
+    def block_copies(j, i, slot):
+        columns = rows_at(i * 1024 + j * 256, 256, 256)
+        return [
+            pltpu.make_async_copy(s.gblock.at[slot], g_all.at[:, columns], s.block_sem.at[slot, 0]),
+            pltpu.make_async_copy(s.dblock.at[slot], d_all.at[:, columns], s.block_sem.at[slot, 1]),
+        ]
+
+    for j in range(4):
+        ready(12 + j)
+
+        def mlp(i, j=j):
+            slot = lax.rem(i, 2)
+            columns = rows_at(i * 1024 + j * 256, 256, 256)
+            if j > 0:
+                for copy in block_copies(j, i, slot):
+                    copy.wait()
+            else:
+                @pl.when(i >= 2)
+                def _():
+                    for copy in block_copies(j, i, slot):
+                        copy.wait()
+
+            s.ublock[...] = dot_nn(s.h2[...], s.v_up[:, columns])
+            bias = s.v_small[i, 12 + j:13 + j, :]
+
+            def hidden(r):
+                p = rows_at(r * 64, 64, 64)
+                value = s.ublock[p, :] + bias
+                cdf = normal_cdf(value)
+                pdf = jnp.exp(-0.5 * value * value) * 0.3989422804014327
+                s.gblock[slot, p, :] = (value * cdf).astype(BF16)
+                s.dblock[slot, p, :] = cdf + value * pdf
+
+            loop(8, hidden)
+            for copy in block_copies(j, i, slot):
+                copy.start()
+
+            def out(n):
+                wide = rows_at(n * 256, 256, 256)
+                s.sum_a[:, wide] += dot_nn(s.gblock[slot], s.v_down[columns, wide])
+
+            loop(4, out)
+
+        loop(4, mlp)
+
+    save("sum3", s.sum_a).start()
+    normalize(s.sum_a, 2, s.y, True)
+    save("y", s.y).start()
+    for copy in block_copies(3, 2, 0) + block_copies(3, 3, 1) + cot_copies():
+        copy.wait()
+    for k in range(16):
+        for copy in weight_saves(k):
+            copy.wait()
+    ends = dict(
+        x=s.x, q=s.q, k=s.k, v=s.v, o=s.o, h1=s.h1, q2=s.q2, k2=s.k2, v2=s.v2, o2=s.o2, h2=s.h2,
+        sum2=s.sum_b, sum3=s.sum_a, y=s.y,
+    )
+    for name, ref in ends.items():
+        save(name, ref).wait()
+
+
+def forward(w_in, w_out, w_up, w_down, small, tok, cot, enc, mask):
+    any_space = pl.BlockSpec(memory_space=pl.ANY)
+    in_vmem = pl.BlockSpec(memory_space=pltpu.VMEM)
+    wide = {"sum1", "sum2", "sum3"}
+    return pl.pallas_call(
+        forward_kernel,
+        out_shape=(
+            jax.ShapeDtypeStruct((6, 1024, 1024), BF16),
+            jax.ShapeDtypeStruct((2, 1024, 1024), BF16),
+            jax.ShapeDtypeStruct((1024, 4096), BF16),
+            jax.ShapeDtypeStruct((4096, 1024), BF16),
+            jax.ShapeDtypeStruct((4, 128, 1024), BF16),
+            jax.ShapeDtypeStruct((16, 1024), F32),
+            jax.ShapeDtypeStruct((512, 4096), BF16),
+            jax.ShapeDtypeStruct((512, 4096), F32),
+        ) + tuple(
+            jax.ShapeDtypeStruct((256 if name in ("k2", "v2") else 512, 1024), F32 if name in wide else BF16)
+            for name in SAVED
+        ),
+        in_specs=[any_space] * 8 + [in_vmem],
+        out_specs=(any_space,) * 5 + (in_vmem,) + (any_space,) * 17,
+        scratch_shapes=list(FORWARD_SCRATCH.values()),
+        compiler_params=pltpu.CompilerParams(
+            collective_id=2, has_side_effects=True, vmem_limit_bytes=62 << 20
+        ),
+    )(w_in, w_out, w_up, w_down, small, tok, cot, enc, mask)
+
+
+def sum_plain(*parts):
+    dims = (1, 1, 1, 1, 1, 0, 0, 0, 0)
+    scattered = [
+        lax.psum_scatter(part.astype(jnp.bfloat16), "shard", scatter_dimension=dim, tiled=True)
+        for part, dim in zip(parts, dims)
+    ]
+    return tuple(lax.psum(part, "rep").astype(jnp.float32) for part in scattered)
+
+
+def fast_layer(
+    sent_tokens, sent_grads, encoder, length, owner_row, attn_in, attn_out, attn_bias,
+    norm_gain, norm_bias, mlp_in, mlp_bias_in, mlp_out, mlp_bias_out,
+):
+    packed = jnp.concatenate(
+        [attn_bias, norm_gain, norm_bias, mlp_bias_in.reshape(4, 256), mlp_bias_out[None],
+         jnp.zeros((7, 256), BF16)], axis=0,
+    ).astype(F32)
+    mask = jnp.broadcast_to(
+        (jnp.arange(512, dtype=jnp.int32) < length).astype(F32)[:, None], (512, 128)
+    )
+    full_in, full_out, up_full, down_full, cot, vectors, g_all, d_all, *saved = forward(
+        attn_in, attn_out, mlp_in, mlp_out, packed, sent_tokens, sent_grads, encoder, mask
+    )
+    saved = dict(zip(SAVED, saved))
+    loads = dict(
+        x1=saved["x"], q1=saved["q"], k1=saved["k"], v1=saved["v"], o1=saved["o"], h1=saved["h1"],
+        q2=saved["q2"], k2=saved["k2"], v2=saved["v2"], o2=saved["o2"], h2=saved["h2"], e1=encoder,
+        cot=cot.reshape(512, 1024), sum1=saved["sum1"], sum2=saved["sum2"], sum3=saved["sum3"],
+    )
+    total, small_total, encoder_grad, back_blocks, grad_blocks, _ = backward(
+        loads, d_all, g_all, full_in, full_out, up_full, down_full, vectors, saved["y"], mask
+    )
+    total = total.astype(F32)
+    pairs = total[:16].reshape(8, 2, 128, 1024)
+    return (
+        pick_blocks(back_blocks, owner_row),
+        pick_blocks(grad_blocks, owner_row),
+        encoder_grad[None],
+        jnp.concatenate([total[26:], total[18:24]]).reshape(6, 256, 1024),
+        jnp.concatenate([total[24:26], total[16:18]]).reshape(2, 256, 1024),
+        small_total[:6],
+        small_total[6:9],
+        small_total[9:12],
+        pairs[:, 1].reshape(8, 128, 2, 4, 128).transpose(2, 1, 3, 0, 4).reshape(256, 4096),
+        small_total[12:16].reshape(1024),
+        pairs[:, 0].reshape(1024, 1024),
+        small_total[16],
+    )
+
+
 def local(
     tokens,
     enc_states,
@@ -176,16 +1354,17 @@
     sequence_at = jnp.sum(jnp.where(matches, slot_ids[None, :], 0), axis=1)
     my_sequence = jnp.sum(jnp.where(slot_ids == my_index, sequence_at, 0))
     my_length = jnp.sum(jnp.where(slot_ids == my_sequence, lengths[0], 0))
-    sent_tokens = jnp.take(tokens, sequence_at, axis=0)
-    sent_grads = jnp.take(cotangent, sequence_at, axis=0)
+    sent_tokens = pick_blocks(tokens, sequence_at)
+    sent_grads = pick_blocks(cotangent, sequence_at)
+    if (lax.axis_size("rep"), groups) == (8, 4):
+        return fast_layer(
+            sent_tokens, sent_grads, enc_states[0], my_length, owner_row, attn_in, attn_out, attn_bias,
+            norm_gain, norm_bias, mlp_in, mlp_bias_in, mlp_out, mlp_bias_out,
+        )
     got_tokens, got_grads = (
         lax.all_to_all(sent_tokens, "shard", split_axis=0, concat_axis=1, tiled=True),
         lax.all_to_all(sent_grads, "shard", split_axis=0, concat_axis=1, tiled=True),
     )
-    inputs = got_tokens[0]
-    row_count = inputs.shape[0]
-    row_mask = (jnp.arange(row_count, dtype=jnp.int32) < my_length).astype(jnp.float32)[:, None]
-    encoder = enc_states[0]
     full_in, full_out, full_bias, full_gain, full_shift = (
         lax.all_gather(attn_in, "shard", axis=1, tiled=True),
         lax.all_gather(attn_out, "shard", axis=1, tiled=True),
@@ -196,6 +1375,17 @@
     bias_rows = full_bias.astype(jnp.float32)
     gain_rows = full_gain.astype(jnp.float32)
     shift_rows = full_shift.astype(jnp.float32)
+    up_full, up_bias, down_full, down_bias = (
+        lax.all_gather(mlp_in, "shard", axis=0, tiled=True),
+        lax.all_gather(mlp_bias_in, "shard", axis=0, tiled=True),
+        lax.all_gather(mlp_out, "shard", axis=0, tiled=True),
+        lax.all_gather(mlp_bias_out, "shard", axis=0, tiled=True),
+    )
+    in_back, out_back, up_back, down_back = full_in, full_out, up_full, down_full
+    inputs = got_tokens[0]
+    row_count = inputs.shape[0]
+    row_mask = (jnp.arange(row_count, dtype=jnp.int32) < my_length).astype(jnp.float32)[:, None]
+    encoder = enc_states[0]
     projected = jnp.einsum("rd,wde->wre", inputs, full_in[:3], preferred_element_type=jnp.float32)
     queries = (projected[0] + bias_rows[0]).astype(jnp.bfloat16)
     keys = projected[1].astype(jnp.bfloat16)
@@ -214,26 +1404,16 @@
     second_sum = first_norm + (matmul(cross_context, full_out[1]) + bias_rows[5])
     second_norm = layer_norm(second_sum, gain_rows[1], shift_rows[1])
     second_low = second_norm.astype(jnp.bfloat16)
-    up_full, up_bias, down_full, down_bias = (
-        lax.all_gather(mlp_in, "shard", axis=0, tiled=True),
-        lax.all_gather(mlp_bias_in, "shard", axis=0, tiled=True),
-        lax.all_gather(mlp_out, "shard", axis=0, tiled=True),
-        lax.all_gather(mlp_bias_out, "shard", axis=0, tiled=True),
-    )
     hidden_pre = matmul(second_low, up_full) + up_bias.astype(jnp.float32)
     hidden_low = gelu_exact(hidden_pre).astype(jnp.bfloat16)
     third_sum = second_norm + (matmul(hidden_low, down_full) + down_bias.astype(jnp.float32))
     result = (layer_norm(third_sum, gain_rows[2], shift_rows[2]) * row_mask).astype(jnp.bfloat16)
     back_blocks = lax.all_to_all(result[None], "shard", split_axis=1, concat_axis=0, tiled=True)
-    output = jnp.take(back_blocks, owner_row, axis=0)
+    output = pick_blocks(back_blocks, owner_row)
     out_grad = got_grads[0].astype(jnp.float32) * row_mask
     third_grad, third_gain_grad, third_shift_grad = jax.vjp(
         layer_norm, third_sum, gain_rows[2], shift_rows[2]
     )[1](out_grad)
-    up_back, down_back = (
-        lax.all_gather(mlp_in, "shard", axis=0, tiled=True),
-        lax.all_gather(mlp_out, "shard", axis=0, tiled=True),
-    )
     down_grad_in = third_grad.astype(jnp.bfloat16)
     grad_down = contract_rows(hidden_low, down_grad_in)
     grad_down_bias = column_sum(down_grad_in)
@@ -242,27 +1422,9 @@
     grad_up = contract_rows(second_low, hidden_pre_grad)
     grad_up_bias = column_sum(hidden_pre_grad)
     second_norm_grad = third_grad + contract_cols(hidden_pre_grad, up_back)
-    mlp_parts = (
-        lax.psum_scatter(
-            grad_up.astype(jnp.bfloat16), "shard", scatter_dimension=0, tiled=True
-        ).astype(jnp.float32),
-        lax.psum_scatter(
-            grad_up_bias.astype(jnp.bfloat16), "shard", scatter_dimension=0, tiled=True
-        ).astype(jnp.float32),
-        lax.psum_scatter(
-            grad_down.astype(jnp.bfloat16), "shard", scatter_dimension=0, tiled=True
-        ).astype(jnp.float32),
-        lax.psum_scatter(
-            grad_down_bias.astype(jnp.bfloat16), "shard", scatter_dimension=0, tiled=True
-        ).astype(jnp.float32),
-    )
     second_grad, second_gain_grad, second_shift_grad = jax.vjp(
         layer_norm, second_sum, gain_rows[1], shift_rows[1]
     )[1](second_norm_grad)
-    in_back, out_back = (
-        lax.all_gather(attn_in, "shard", axis=1, tiled=True),
-        lax.all_gather(attn_out, "shard", axis=1, tiled=True),
-    )
     cross_out_grad = second_grad.astype(jnp.bfloat16)
     grad_cross_out = contract_rows(cross_context, cross_out_grad)
     grad_cross_out_bias = column_sum(cross_out_grad)
@@ -307,7 +1469,7 @@
         + contract_cols(value_low, in_back[2])
     ).astype(jnp.bfloat16)
     grad_blocks = lax.all_to_all(input_grad[None], "shard", split_axis=1, concat_axis=0, tiled=True)
-    grad_tokens = jnp.take(grad_blocks, owner_row, axis=0)
+    grad_tokens = pick_blocks(grad_blocks, owner_row)
     grad_in_full = jnp.stack(
         [grad_query, grad_key, grad_value, grad_cross_query, grad_cross_key, grad_cross_value]
     )
@@ -324,33 +1486,9 @@
     )
     grad_gain_full = jnp.stack([first_gain_grad, second_gain_grad, third_gain_grad])
     grad_shift_full = jnp.stack([first_shift_grad, second_shift_grad, third_shift_grad])
-    attn_parts = (
-        lax.psum_scatter(
-            grad_in_full.astype(jnp.bfloat16), "shard", scatter_dimension=1, tiled=True
-        ).astype(jnp.float32),
-        lax.psum_scatter(
-            grad_out_full.astype(jnp.bfloat16), "shard", scatter_dimension=1, tiled=True
-        ).astype(jnp.float32),
-        lax.psum_scatter(
-            grad_bias_full.astype(jnp.bfloat16), "shard", scatter_dimension=1, tiled=True
-        ).astype(jnp.float32),
-        lax.psum_scatter(
-            grad_gain_full.astype(jnp.bfloat16), "shard", scatter_dimension=1, tiled=True
-        ).astype(jnp.float32),
-        lax.psum_scatter(
-            grad_shift_full.astype(jnp.bfloat16), "shard", scatter_dimension=1, tiled=True
-        ).astype(jnp.float32),
-    )
-    summed = (
-        lax.psum(attn_parts[0].astype(jnp.bfloat16), "rep").astype(jnp.float32),
-        lax.psum(attn_parts[1].astype(jnp.bfloat16), "rep").astype(jnp.float32),
-        lax.psum(attn_parts[2].astype(jnp.bfloat16), "rep").astype(jnp.float32),
-        lax.psum(attn_parts[3].astype(jnp.bfloat16), "rep").astype(jnp.float32),
-        lax.psum(attn_parts[4].astype(jnp.bfloat16), "rep").astype(jnp.float32),
-        lax.psum(mlp_parts[0].astype(jnp.bfloat16), "rep").astype(jnp.float32),
-        lax.psum(mlp_parts[1].astype(jnp.bfloat16), "rep").astype(jnp.float32),
-        lax.psum(mlp_parts[2].astype(jnp.bfloat16), "rep").astype(jnp.float32),
-        lax.psum(mlp_parts[3].astype(jnp.bfloat16), "rep").astype(jnp.float32),
+    summed = sum_plain(
+        grad_in_full, grad_out_full, grad_bias_full, grad_gain_full, grad_shift_full,
+        grad_up, grad_up_bias, grad_down, grad_down_bias,
     )
     return (
         output,

time: 1020 us -> 469 us (0.46)
  waiting for transfers between devices: 527 us -> 0 us
  Pallas kernels: 0 us -> 403 us
  matrix products: 214 us -> 0 us
  blocking collectives: 103 us -> 0 us
  other arithmetic: 69 us -> 13.1 us
  local copies, waits for them, and re-layouts: 68.3 us -> 35.9 us
  starting transfers between devices: 17.2 us -> 0 us
    pallas_call x0 -> x2, Pallas kernels: none -> 403 us  [the longest x1 265 us: backward(): pl.pallas_call(back_kernel, out_shape=(jax.ShapeDtypeStruct((CHUNKS, ROWS...]
    psum x1 -> x0, waiting for transfers between devices: 220 us -> none  [local(): lax.psum(attn_parts[0].astype(jnp.bfloat16), 'rep').astype(jnp.float32)]
    dot_general x83 -> x0, matrix products: 214 us -> none  [the longest x5 51.6 us: matmul(): return jnp.dot(left, right, preferred_element_type=jnp.float32)]
    reduce_scatter x5 -> x0, waiting for transfers between devices: 200 us -> none  [the longest x1 102 us: local(): lax.psum_scatter(grad_in_full.astype(jnp.bfloat16), 'shard', scatter_dime...]
    all_gather x4 -> x0, waiting for transfers between devices: 104 us -> none  [the longest x1 44.5 us: local(): lax.all_gather(attn_in, 'shard', axis=1, tiled=True)]
    all_gather x5 -> x0, blocking collectives: 43.5 us -> none  [the longest x1 23 us: local(): lax.all_gather(attn_bias, 'shard', axis=1, tiled=True)]
    psum x1 -> x0, blocking collectives: 39.4 us -> none  [local(): lax.psum(attn_parts[2].astype(jnp.bfloat16), 'rep').astype(jnp.float32)]
    unnamed x143 -> x25, local copies, waits for them, and re-layouts: 29.9 us -> 1.46 us
  transfers between devices with their start and end apart: 16 -> 0, of which waited for: 7 -> 0; matrix products, arithmetic and copies ran while one was open for 24% -> 0% of each run, Pallas kernels for 0% -> 0%
where the time goes in v1:
time: 469 us; the launch traced here: 468 us
  Pallas kernels  403 us (86%)
  local copies, waits for them, and re-layouts  35.9 us (8%)
  between operations  16.4 us (3%)
  other arithmetic  13.1 us (3%)
    pallas_call x1, Pallas kernels, backward(): pl.pallas_call(back_kernel, out_shape=(jax.ShapeDtypeStruct((CHUNKS, ROWS...  265 us
    pallas_call x1, Pallas kernels, forward(): pl.pallas_call(forward_kernel, out_shape=(jax.ShapeDtypeStruct((6, 1024,...  138 us
    another operation x2, local copies, waits for them, and re-layouts, fast_layer(): pairs[:, 1].reshape(8, 128, 2, 4, 128).transpose(2, 1, 3, 0, 4)  12.2 us

profile of v1, /device:TPU:0, one launch (start us, length us, event | category | flops | bytes accessed | tf_op | source)
XLA Modules:
  0.0 468.1 jit_solution(8155471256266591225)
XLA Ops:
  0.6 0.8 select_reduce_fusion
  1.4 0.6 fusion.8
  9.8 0.0 copy-start.9
  9.8 0.0 copy-start.8
  9.8 0.0 copy-start.10
  9.8 0.0 copy-start.5
  9.8 0.0 copy-start.6
  9.8 0.0 copy-start.7
  9.8 1.8 constant_dynamic-slice_fusion.11
  11.6 1.1 pad_maximum_fusion.3.refs_6_
  12.7 1.1 pad_maximum_fusion.2.refs_5_
  13.8 0.6 fusion.1
  14.4 0.0 copy-done.9
  14.5 1.3 fusion.2
  15.7 0.6 fusion
  16.4 0.8 broadcast_in_dim.39.refs_8_.refs_24_
  17.2 0.0 copy-done.8
  17.2 0.0 copy-done.10
  17.3 0.0 copy-done.5
  17.3 0.0 copy-done.6
  17.3 0.0 copy-done.7
  17.3 0.1 concatenate.21
  17.4 0.6 convert_element_type.13.refs_4_
  18.0 138.0 %shard_map.229 = (bf16[6,1024,1024]{2,1,0:T(8,128)(2,1)}, bf16[2,1024,1024]{2,1,0:T(8,128)(2,1)}, bf16[1024,4096]{1,0:T(8,128)(2,1)}, bf16[4096,1024]{1,0:T(8,12...) custom-call(bf16[6,256,1024]{2,1,0:T(8,128)(2,1)} %refs_0_.1, ...), custom_call_target="tpu_custom_call" | custom-call | tf_op jit(solution)/shard_map/pallas_call | solution.py:1259
  156.0 264.7 %shard_map.230 = (bf16[32,128,1024]{2,1,0:T(8,128)(2,1)}, f32[24,256]{1,0:T(8,128)}, bf16[256,1024]{1,0:T(8,128)(2,1)}, bf16[4,128,1024]{2,1,0:T(8,128)(2,1)}, b...) custom-call(bf16[512,1024]{1,0:T(8,128)(2,1)} %get-tuple-element.40.refs_0_, ...), custom_call_target="tpu_custom_call" | custom-call | tf_op jit(solution)/shard_map/pallas_call | solution.py:852
  420.7 3.2 slice.96
  424.0 4.2 fusion.3
  428.2 5.6 %reshape_squeeze.6 = f32[8,128,2,4,128]{4,3,2,1,0:T(4,128)} reshape(f32[8,1,128,1024]{3,2,1,0:T(8,128)} %get-tuple-element.69) | data formatting | bytes 8388608 | tf_op jit(solution)/shard_map/reshape;squeeze | solution.py:1326
  433.8 6.6 %copy.30 = f32[8,128,2,4,128]{4,0,3,1,2:T(8,128)} copy(f32[8,128,2,4,128]{4,3,2,1,0:T(4,128)} %reshape_squeeze.6) | data formatting | bytes 8388608 | tf_op jit(solution)/shard_map/reshape;squeeze | solution.py:1326
  440.4 4.9 %reshape.63 = f32[256,4096]{1,0:T(8,128)} reshape(f32[2,128,4,8,128]{4,3,2,1,0:T(8,128)} %bitcast.30) | data formatting | bytes 8388608 | tf_op jit(solution)/shard_map/reshape | solution.py:1326
  445.3 1.4 fusion.4
  446.8 1.5 pad_maximum_fusion.1
  448.2 2.6 fusion.5
  450.9 0.0 copy-start.4
  450.9 0.0 copy-start.1
  450.9 3.3 pad_maximum_fusion
  454.2 0.0 copy-start
  454.2 0.0 copy-done.4
  454.2 0.6 fusion.7
  462.5 0.0 copy-done.1
  462.5 0.0 copy-start.3
  462.5 0.0 copy-start.2
  462.6 0.1 constant_dynamic-slice_fusion.3
  462.6 1.1 pad_maximum_fusion.5
  463.7 0.0 copy-done
  463.8 0.1 constant_dynamic-slice_fusion.7
  463.8 1.1 pad_maximum_fusion.4
  464.9 0.0 copy-done.3
  464.9 0.6 fusion.6
  465.5 0.6 copy.28
  466.1 0.6 slice.84
  466.7 0.6 slice.91
  467.3 0.0 copy-done.2
  467.3 0.8 copy.32
  (4 shorter events, 0.0 us)
Async XLA Ops:
  9.8 4.7 copy-start.9
  9.8 7.4 %copy-start.8 = (bf16[1024]{0:T(1024)(128)(2,1)S(1)}, bf16[1024]{0:T(1024)(128)(2,1)}, u32[]{:S(2)}) copy-start(bf16[1024]{0:T(1024)(128)(2,1)} %param.25) | copy-start | bytes 6148
  9.8 7.4 %copy-start.10 = (bf16[256]{0:T(256)(128)(2,1)S(1)}, bf16[256]{0:T(256)(128)(2,1)}, u32[]{:S(2)}) copy-start(bf16[256]{0:T(256)(128)(2,1)} %param.27) | copy-start | bytes 1540
  9.8 7.4 %copy-start.5 = (bf16[6,256]{1,0:T(8,128)(2,1)S(1)}, bf16[6,256]{1,0:T(8,128)(2,1)}, u32[]{:S(2)}) copy-start(bf16[6,256]{1,0:T(8,128)(2,1)} %param.21) | copy-start | bytes 9220
  9.8 7.4 %copy-start.6 = (bf16[3,256]{1,0:T(4,128)(2,1)S(1)}, bf16[3,256]{1,0:T(4,128)(2,1)}, u32[]{:S(2)}) copy-start(bf16[3,256]{1,0:T(4,128)(2,1)} %param.22) | copy-start | bytes 4612
  9.8 7.4 %copy-start.7 = (bf16[3,256]{1,0:T(4,128)(2,1)S(1)}, bf16[3,256]{1,0:T(4,128)(2,1)}, u32[]{:S(2)}) copy-start(bf16[3,256]{1,0:T(4,128)(2,1)} %param.23) | copy-start | bytes 4612
  450.9 3.3 copy-start.4
  450.9 11.7 %copy-start.1 = (bf16[4,128,1024]{2,1,0:T(8,128)(2,1)S(1)}, bf16[4,128,1024]{2,1,0:T(8,128)(2,1)}, u32[]{:S(2)}) copy-start(bf16[4,128,1024]{2,1,0:T(8,128)(2,1)} %get-tuple-element.64) | copy-start | bytes 3145732
  454.2 9.6 %copy-start = (bf16[4,128,1024]{2,1,0:T(8,128)(2,1)S(1)}, bf16[4,128,1024]{2,1,0:T(8,128)(2,1)}, u32[]{:S(2)}) copy-start(bf16[4,128,1024]{2,1,0:T(8,128)(2,1)} %get-tuple-element.63) | copy-start | bytes 3145732
  462.5 2.4 copy-start.3
  462.5 4.8 %copy-start.2 = (bf16[256,1024]{1,0:T(8,128)(2,1)S(1)}, bf16[256,1024]{1,0:T(8,128)(2,1)}, u32[]{:S(2)}) copy-start(bf16[256,1024]{1,0:T(8,128)(2,1)} %get-tuple-element.65) | copy-start | bytes 1572868

commit v2 on v1

--- a/solution.py
+++ b/solution.py
@@ -190,7 +190,7 @@
 
 F32, BF16 = jnp.float32, jnp.bfloat16
 RING = 8
-LAGS = (0, 2, 3, 4, 5, 6, 7)
+LAGS = (0, 1, 3, 4, 5, 6, 7)
 
 
 def dot_over(left, right, a, b):
@@ -834,11 +834,14 @@
         s.low[:, p] = (s.dz[:, p] + dot_nt(s.dvb[...], s.wb[1, p, :])).astype(BF16)
 
     loop(4, last)
-    for copy in row_copies(1, s.low, grad_back):
-        copy.start()
-
     def drain(i):
         reducer.tick(31 + i)
+
+        @pl.when(i == LAGS[1])
+        def _():
+            for copy in row_copies(1, s.low, grad_back):
+                copy.start()
+
         reducer.small_steps(i)
 
     loop(max(9, CHUNKS + LAGS[-1] - 31), drain)
@@ -873,6 +876,8 @@
     v_out=pltpu.VMEM((2, 1024, 1024), BF16),
     v_up=pltpu.VMEM((1024, 4096), BF16),
     v_down=pltpu.VMEM((4096, 1024), BF16),
+    small=pltpu.VMEM((24, 256), F32),
+    s_tok=pltpu.VMEM((4, 128, 1024), BF16),
     v_small=pltpu.VMEM((4, 24, 256), F32),
     vec=pltpu.VMEM((24, 1024), F32),
     x=pltpu.VMEM((512, 1024), BF16),
@@ -1022,10 +1027,15 @@
 
 
 def forward_kernel(*refs):
-    w_in, w_out, w_up, w_down, small, tok, cot, enc, mask = refs[:9]
-    f_in, f_out, f_up, f_down, f_cot, gains, g_all, d_all = refs[9:17]
-    saved = dict(zip(SAVED, refs[17:32]))
-    s = types.SimpleNamespace(**dict(zip(FORWARD_SCRATCH, refs[32:])))
+    owner, lengths, bias, gain_in, shift_in, up_bias, down_bias, tok_in, cot_in = refs[:9]
+    w_in, w_out, w_up, w_down, enc = refs[9:14]
+    f_in, f_out, f_up, f_down, f_cot, gains, mask, g_all, d_all = refs[14:23]
+    saved = dict(zip(SAVED, refs[23:38]))
+    s = types.SimpleNamespace(**dict(zip(FORWARD_SCRATCH, refs[38:])))
+    sequence_at = [
+        jnp.clip(sum(jnp.where(owner[0, j] == i, j, 0) for j in range(4)), 0, 3) for i in range(4)
+    ]
+    small, tok = s.small, s.s_tok
     full = (s.v_in, s.v_out, s.v_up, s.v_down)
     gather = Gatherer(s, (w_in, w_out, w_up, w_down), full)
     mine, (_, _, x, c) = gather.mine, gather.at
@@ -1033,6 +1043,14 @@
 
     def rows_of(index):
         return rows_at(index * 128, 128, 128)
+
+    def arrange(source, target):
+        for i in range(4):
+            def block(n, i=i):
+                p = rows_at(n * 32, 32, 32)
+                target[i, p, :] = source[sequence_at[i], p, :]
+
+            loop(4, block)
 
     def token_copies():
         return [
@@ -1048,13 +1066,21 @@
 
     def cot_copies():
         return [
-            remote(cot.at[slot], f_cot.at[mine], s.t_send.at[1, i], s.t_recv.at[1, i], peer)
+            remote(tok.at[slot], f_cot.at[mine], s.t_send.at[1, i], s.t_recv.at[1, i], peer)
             for i, (peer, slot) in enumerate(peers)
-        ] + [pltpu.make_async_copy(cot.at[mine], f_cot.at[mine], s.t_own.at[2])]
+        ] + [pltpu.make_async_copy(tok.at[mine], f_cot.at[mine], s.t_own.at[2])]
 
     enc_copy = pltpu.make_async_copy(enc, s.e, s.t_own.at[3])
+    enc_copy.start()
+    arrange(tok_in, s.s_tok)
+    small[...] = jnp.zeros_like(small)
+    small[0:6, :] = bias[...].astype(F32)
+    small[6:9, :] = gain_in[...].astype(F32)
+    small[9:12, :] = shift_in[...].astype(F32)
+    for i in range(4):
+        small[12 + i:13 + i, :] = up_bias[:, i * 256:(i + 1) * 256].astype(F32)
+    small[16:17, :] = down_bias[...].astype(F32)
     gather.greet()
-    enc_copy.start()
     gather.advance(-2)
     for copy in token_copies():
         copy.start()
@@ -1136,6 +1162,11 @@
                 context = context + dot_nn(weights.astype(BF16), value * head_mask)
             o_ref[rows, lanes] = context.astype(BF16)
 
+    length = jnp.int32(0)
+    for i in range(4):
+        here = sum(jnp.where(sequence_at[i] == j, lengths[0, j], 0) for j in range(4))
+        length = length + jnp.where(mine == i, here, 0)
+    mask[...] = (lax.broadcasted_iota(jnp.int32, (512, 128), 0) < length).astype(F32)
     ready(0)
     for copy in token_copies():
         copy.wait()
@@ -1180,6 +1211,7 @@
     ready(10)
     normalize(s.sum_b, 1, s.h2, False)
     save("h2", s.h2).start()
+    arrange(cot_in, s.s_tok)
     for copy in cot_copies():
         copy.start()
     save("sum1", s.sum_a).wait()
@@ -1252,9 +1284,10 @@
         save(name, ref).wait()
 
 
-def forward(w_in, w_out, w_up, w_down, small, tok, cot, enc, mask):
+def forward(*operands):
     any_space = pl.BlockSpec(memory_space=pl.ANY)
     in_vmem = pl.BlockSpec(memory_space=pltpu.VMEM)
+    in_smem = pl.BlockSpec(memory_space=pltpu.SMEM)
     wide = {"sum1", "sum2", "sum3"}
     return pl.pallas_call(
         forward_kernel,
@@ -1265,19 +1298,20 @@
             jax.ShapeDtypeStruct((4096, 1024), BF16),
             jax.ShapeDtypeStruct((4, 128, 1024), BF16),
             jax.ShapeDtypeStruct((16, 1024), F32),
+            jax.ShapeDtypeStruct((512, 128), F32),
             jax.ShapeDtypeStruct((512, 4096), BF16),
             jax.ShapeDtypeStruct((512, 4096), F32),
         ) + tuple(
             jax.ShapeDtypeStruct((256 if name in ("k2", "v2") else 512, 1024), F32 if name in wide else BF16)
             for name in SAVED
         ),
-        in_specs=[any_space] * 8 + [in_vmem],
-        out_specs=(any_space,) * 5 + (in_vmem,) + (any_space,) * 17,
+        in_specs=[in_smem] * 2 + [in_vmem] * 7 + [any_space] * 5,
+        out_specs=(any_space,) * 5 + (in_vmem,) * 2 + (any_space,) * 17,
         scratch_shapes=list(FORWARD_SCRATCH.values()),
         compiler_params=pltpu.CompilerParams(
             collective_id=2, has_side_effects=True, vmem_limit_bytes=62 << 20
         ),
-    )(w_in, w_out, w_up, w_down, small, tok, cot, enc, mask)
+    )(*operands)
 
 
 def sum_plain(*parts):
@@ -1289,19 +1323,90 @@
     return tuple(lax.psum(part, "rep").astype(jnp.float32) for part in scattered)
 
 
+def finish_kernel(owner, total, small_total, out_back, grad_back, *refs):
+    out, grad_tok, g_in, g_out, g_up, g_down, g_bias, g_gain, g_shift, g_up_bias, g_down_bias, w_in, w_out, w_up, w_down, sem, row_sem = refs
+    copies = []
+    for i in range(4):
+        for j, (src, dst) in enumerate(((out_back, out), (grad_back, grad_tok))):
+            copies.append(pltpu.make_async_copy(src.at[jnp.clip(owner[0, i], 0, 3)], dst.at[i], row_sem.at[i, j]))
+            copies[-1].start()
+    g_bias[...] = small_total[0:6, :]
+    g_gain[...] = small_total[6:9, :]
+    g_shift[...] = small_total[9:12, :]
+    for i in range(4):
+        g_up_bias[:, i * 256:(i + 1) * 256] = small_total[12 + i:13 + i, :]
+    g_down_bias[...] = small_total[16:17, :]
+
+    def widen(k, dst):
+        def block(i):
+            p = rows_at(i * 32, 32, 32)
+            dst(p, total[k, p, :].astype(F32))
+
+        loop(4, block)
+
+    def send(src, dst, index):
+        copies.append(pltpu.make_async_copy(src, dst, sem.at[index]))
+        copies[-1].start()
+
+    for j in range(8):
+        def up(p, value):
+            for half in (0, 1):
+                rows = rows_at(p.start + half * 128, 32, 32)
+                for c in range(4):
+                    w_up[rows, c * 1024 + j * 128:c * 1024 + j * 128 + 128] = (
+                        value[:, half * 512 + c * 128:half * 512 + c * 128 + 128]
+                    )
+
+        widen(2 * j + 1, up)
+        rows = pl.ds(j * 128, 128)
+
+        def down(p, value):
+            w_down[rows_at(j * 128 + p.start, 32, 32), :] = value
+
+        widen(2 * j, down)
+        send(w_down.at[rows, :], g_down.at[rows, :], j)
+    send(w_up, g_up, 8)
+    order = [(g_out, w_out, 1, 16), (g_in, w_in, 3, 18), (g_in, w_in, 4, 20), (g_in, w_in, 5, 22),
+             (g_out, w_out, 0, 24), (g_in, w_in, 0, 26), (g_in, w_in, 1, 28), (g_in, w_in, 2, 30)]
+    for n, (dst, held, index, chunk) in enumerate(order):
+        for half in (0, 1):
+            def place_rows(p, value):
+                held[index, rows_at(half * 128 + p.start, 32, 32), :] = value
+
+            widen(chunk + half, place_rows)
+        send(held.at[index], dst.at[index], 9 + n)
+    for copy in copies:
+        copy.wait()
+
+
+def finish(owner, total, small_total, out_back, grad_back):
+    any_space = pl.BlockSpec(memory_space=pl.ANY)
+    in_vmem = pl.BlockSpec(memory_space=pltpu.VMEM)
+    narrow = [(6, 256), (3, 256), (3, 256), (1, 1024), (1, 256)]
+    wide = [(6, 256, 1024), (2, 256, 1024), (256, 4096), (1024, 1024)]
+    return pl.pallas_call(
+        finish_kernel,
+        out_shape=tuple(
+            [jax.ShapeDtypeStruct((4, 128, 1024), BF16)] * 2
+            + [jax.ShapeDtypeStruct(shape, F32) for shape in wide]
+            + [jax.ShapeDtypeStruct(shape, F32) for shape in narrow]
+        ),
+        in_specs=[pl.BlockSpec(memory_space=pltpu.SMEM)] + [in_vmem] * 4,
+        out_specs=tuple([any_space] * 6 + [in_vmem] * 5),
+        scratch_shapes=[pltpu.VMEM(shape, F32) for shape in wide]
+        + [pltpu.SemaphoreType.DMA((17,)), pltpu.SemaphoreType.DMA((4, 2))],
+        compiler_params=pltpu.CompilerParams(vmem_limit_bytes=60 << 20),
+    )(owner, total, small_total, out_back, grad_back)
+
+
 def fast_layer(
-    sent_tokens, sent_grads, encoder, length, owner_row, attn_in, attn_out, attn_bias,
+    tokens, enc_states, cotangent, lengths, owner, attn_in, attn_out, attn_bias,
     norm_gain, norm_bias, mlp_in, mlp_bias_in, mlp_out, mlp_bias_out,
 ):
-    packed = jnp.concatenate(
-        [attn_bias, norm_gain, norm_bias, mlp_bias_in.reshape(4, 256), mlp_bias_out[None],
-         jnp.zeros((7, 256), BF16)], axis=0,
-    ).astype(F32)
-    mask = jnp.broadcast_to(
-        (jnp.arange(512, dtype=jnp.int32) < length).astype(F32)[:, None], (512, 128)
-    )
-    full_in, full_out, up_full, down_full, cot, vectors, g_all, d_all, *saved = forward(
-        attn_in, attn_out, mlp_in, mlp_out, packed, sent_tokens, sent_grads, encoder, mask
+    encoder = enc_states[0]
+    full_in, full_out, up_full, down_full, cot, vectors, mask, g_all, d_all, *saved = forward(
+        owner, lengths, attn_bias, norm_gain, norm_bias, mlp_bias_in.reshape(1, 1024),
+        mlp_bias_out.reshape(1, 256), tokens, cotangent, attn_in, attn_out, mlp_in, mlp_out, encoder,
     )
     saved = dict(zip(SAVED, saved))
     loads = dict(
@@ -1312,21 +1417,12 @@
     total, small_total, encoder_grad, back_blocks, grad_blocks, _ = backward(
         loads, d_all, g_all, full_in, full_out, up_full, down_full, vectors, saved["y"], mask
     )
-    total = total.astype(F32)
-    pairs = total[:16].reshape(8, 2, 128, 1024)
+    out, grad_tokens, g_in, g_out, g_up, g_down, *small = finish(
+        owner, total, small_total, back_blocks, grad_blocks
+    )
     return (
-        pick_blocks(back_blocks, owner_row),
-        pick_blocks(grad_blocks, owner_row),
-        encoder_grad[None],
-        jnp.concatenate([total[26:], total[18:24]]).reshape(6, 256, 1024),
-        jnp.concatenate([total[24:26], total[16:18]]).reshape(2, 256, 1024),
-        small_total[:6],
-        small_total[6:9],
-        small_total[9:12],
-        pairs[:, 1].reshape(8, 128, 2, 4, 128).transpose(2, 1, 3, 0, 4).reshape(256, 4096),
-        small_total[12:16].reshape(1024),
-        pairs[:, 0].reshape(1024, 1024),
-        small_total[16],
+        out, grad_tokens, encoder_grad[None], g_in, g_out, small[0], small[1], small[2],
+        g_up, small[3].reshape(1024), g_down, small[4].reshape(256),
     )
 
 
@@ -1347,6 +1443,11 @@
     mlp_bias_out,
 ):
     groups = lax.axis_size("shard")
+    if (lax.axis_size("rep"), groups) == (8, 4):
+        return fast_layer(
+            tokens, enc_states, cotangent, lengths, owner, attn_in, attn_out, attn_bias,
+            norm_gain, norm_bias, mlp_in, mlp_bias_in, mlp_out, mlp_bias_out,
+        )
     my_index = lax.axis_index("shard")
     owner_row = owner[0]
     slot_ids = jnp.arange(groups, dtype=jnp.int32)
@@ -1356,11 +1457,6 @@
     my_length = jnp.sum(jnp.where(slot_ids == my_sequence, lengths[0], 0))
     sent_tokens = pick_blocks(tokens, sequence_at)
     sent_grads = pick_blocks(cotangent, sequence_at)
-    if (lax.axis_size("rep"), groups) == (8, 4):
-        return fast_layer(
-            sent_tokens, sent_grads, enc_states[0], my_length, owner_row, attn_in, attn_out, attn_bias,
-            norm_gain, norm_bias, mlp_in, mlp_bias_in, mlp_out, mlp_bias_out,
-        )
     got_tokens, got_grads = (
         lax.all_to_all(sent_tokens, "shard", split_axis=0, concat_axis=1, tiled=True),
         lax.all_to_all(sent_grads, "shard", split_axis=0, concat_axis=1, tiled=True),

time: 469 us -> 402 us (0.86)
  local copies, waits for them, and re-layouts: 35.9 us -> 3.3 us
  between operations: 16.4 us -> 0.68 us
  other arithmetic: 13.1 us -> 0 us
  Pallas kernels: 403 us -> 398 us
    pallas_call x1, Pallas kernels: 265 us -> 248 us  [backward(): pl.pallas_call(back_kernel, out_shape=(jax.ShapeDtypeStruct((CHUNKS, ROWS...]
    slice x9 -> x0, local copies, waits for them, and re-layouts: 14.5 us -> none  [the longest x1 4.24 us: fast_layer(): pairs[:, 0].reshape(1024, 1024)]
    another operation x2 -> x0, local copies, waits for them, and re-layouts: 12.2 us -> none  [fast_layer(): pairs[:, 1].reshape(8, 128, 2, 4, 128).transpose(2, 1, 3, 0, 4)]
    pallas_call x0 -> x1, Pallas kernels: none -> 11.3 us  [finish(): pl.pallas_call(finish_kernel, out_shape=tuple([jax.ShapeDtypeStruct((4, 1...]
    concatenate x6 -> x0, other arithmetic: 9.17 us -> none  [the longest x4 4.41 us: pick_blocks(): jnp.concatenate([lax.dynamic_slice_in_dim(blocks, order[i], 1, axis=0) fo...]
where the time goes in v2:
time: 402 us
  Pallas kernels  398 us (99%)
    pallas_call x1, Pallas kernels, backward(): pl.pallas_call(back_kernel, out_shape=(jax.ShapeDtypeStruct((CHUNKS, ROWS...  248 us
    pallas_call x1, Pallas kernels, forward(): pl.pallas_call(forward_kernel, out_shape=(jax.ShapeDtypeStruct((6, 1024,...  139 us
    pallas_call x1, Pallas kernels, finish(): pl.pallas_call(finish_kernel, out_shape=tuple([jax.ShapeDtypeStruct((4, 1...  11.3 us

profile of v2, /device:TPU:0, one launch (start us, length us, event | category | flops | bytes accessed | tf_op | source)
XLA Modules:
  0.0 401.9 jit_solution(6616952750241426748)
XLA Ops:
  0.6 1.2 reshape.40.refs_6_
  1.9 1.3 reshape.39.refs_5_
  3.1 138.8 %shard_map.229 = (bf16[6,1024,1024]{2,1,0:T(8,128)(2,1)}, bf16[2,1024,1024]{2,1,0:T(8,128)(2,1)}, bf16[1024,4096]{1,0:T(8,128)(2,1)}, bf16[4096,1024]{1,0:T(8,12...) custom-call(s32[1,4]{1,0:T(1,128)} %owner.1, ...), custom_call_target="tpu_custom_call" | custom-call | tf_op jit(solution)/shard_map/pallas_call | solution.py:1292
  141.9 247.9 %shard_map.230 = (bf16[32,128,1024]{2,1,0:T(8,128)(2,1)}, f32[24,256]{1,0:T(8,128)}, bf16[256,1024]{1,0:T(8,128)(2,1)}, bf16[4,128,1024]{2,1,0:T(8,128)(2,1)}, b...) custom-call(bf16[512,1024]{1,0:T(8,128)(2,1)} %get-tuple-element.52.refs_0_, ...), custom_call_target="tpu_custom_call" | custom-call | tf_op jit(solution)/shard_map/pallas_call | solution.py:855
  389.8 0.0 copy-start
  389.8 11.3 %shard_map.231 = (bf16[4,128,1024]{2,1,0:T(8,128)(2,1)}, bf16[4,128,1024]{2,1,0:T(8,128)(2,1)}, f32[6,256,1024]{2,1,0:T(8,128)}, f32[2,256,1024]{2,1,0:T(8,128)}...) custom-call(s32[1,4]{1,0:T(1,128)} %owner.1, ...), custom_call_target="tpu_custom_call" | custom-call | tf_op jit(solution)/shard_map/pallas_call | solution.py:1387
  401.1 0.0 copy-done
  401.1 0.8 copy.27
Async XLA Ops:
  389.8 11.3 %copy-start = (bf16[256,1024]{1,0:T(8,128)(2,1)S(1)}, bf16[256,1024]{1,0:T(8,128)(2,1)}, u32[]{:S(2)}) copy-start(bf16[256,1024]{1,0:T(8,128)(2,1)} %get-tuple-element.82) | copy-start | bytes 1572868

commit v3 on v2

--- a/solution.py
+++ b/solution.py
@@ -654,6 +654,14 @@
             for copy in tile_copies(j + 1, 1 - slot):
                 copy.start()
 
+        def down(i):
+            product = dot_tn(s.gt[slot, :, rows_at(i * 256, 256, 256)], s.low[...]).astype(BF16)
+            s.stage[0, 2 * i] = product[:128]
+            s.stage[0, 2 * i + 1] = product[128:]
+
+        loop(2, down)
+        down_save(j).start()
+
         def hidden(i):
             p = rows_at(i * 256, 256, 256)
             grad = dot_nt(s.low[...], s.wd[slot, p, :])
@@ -662,14 +670,12 @@
             s.ub[j, :, p] = jnp.sum(rounded.astype(F32), axis=0, keepdims=True)
 
         loop(2, hidden)
-
-        def down(i):
-            product = dot_tn(s.gt[slot, :, rows_at(i * 256, 256, 256)], s.low[...]).astype(BF16)
-            s.stage[0, 2 * i] = product[:128]
-            s.stage[0, 2 * i + 1] = product[128:]
-
-        loop(2, down)
-        down_save(j).start()
+        down_save(j).wait()
+
+        @pl.when(lax.rem(j, 2) == 0)
+        def _():
+            reducer.tick(3 * j // 2)
+
 
         def up(i):
             product = dot_tn(s.h2[:, rows_at(i * 256, 256, 256)], s.dut[...]).astype(BF16)
@@ -684,9 +690,8 @@
             s.dz[:, p] += dot_nt(s.dut[...], s.wu[slot, p, :])
 
         loop(4, back)
-        down_save(j).wait()
         up_save(j).wait()
-        loop(2 - lax.rem(j, 2), lambda i: reducer.tick((3 * j + 1) // 2 + i))
+        reducer.tick((3 * j + 2) // 2)
 
     loop(8, tile)
     for j in range(8):
@@ -896,42 +901,45 @@
     hf=pltpu.VMEM((512, 1024), F32),
     sum_a=pltpu.VMEM((512, 1024), F32),
     sum_b=pltpu.VMEM((512, 1024), F32),
-    ublock=pltpu.VMEM((512, 256), F32),
-    gblock=pltpu.VMEM((2, 512, 256), BF16),
-    dblock=pltpu.VMEM((2, 512, 256), F32),
-    own_sem=pltpu.SemaphoreType.DMA((16,)),
-    x_send=pltpu.SemaphoreType.DMA((16,)),
-    x_recv=pltpu.SemaphoreType.DMA((16,)),
-    y_send=pltpu.SemaphoreType.DMA((16, 2)),
-    y_recv=pltpu.SemaphoreType.DMA((16, 2)),
-    z_send=pltpu.SemaphoreType.DMA((16, 2)),
-    z_recv=pltpu.SemaphoreType.DMA((16, 2)),
-    c_send=pltpu.SemaphoreType.DMA((16, 2)),
-    c_recv=pltpu.SemaphoreType.DMA((16, 2)),
+    ublock=pltpu.VMEM((512, 512), F32),
+    gblock=pltpu.VMEM((2, 512, 512), BF16),
+    dblock=pltpu.VMEM((2, 512, 512), F32),
+    own_sem=pltpu.SemaphoreType.DMA((16, 4)),
+    x_send=pltpu.SemaphoreType.DMA((16, 4)),
+    x_recv=pltpu.SemaphoreType.DMA((16, 4)),
+    y_send=pltpu.SemaphoreType.DMA((16, 2, 4)),
+    y_recv=pltpu.SemaphoreType.DMA((16, 2, 4)),
+    z_send=pltpu.SemaphoreType.DMA((16, 2, 4)),
+    z_recv=pltpu.SemaphoreType.DMA((16, 2, 4)),
+    c_send=pltpu.SemaphoreType.DMA((16, 2, 4)),
+    c_recv=pltpu.SemaphoreType.DMA((16, 2, 4)),
     t_send=pltpu.SemaphoreType.DMA((3, 3)),
     t_recv=pltpu.SemaphoreType.DMA((3, 3)),
     t_own=pltpu.SemaphoreType.DMA((4,)),
     save_sem=pltpu.SemaphoreType.DMA((16,)),
     weight_sem=pltpu.SemaphoreType.DMA((16,)),
-    block_sem=pltpu.SemaphoreType.DMA((2, 2)),
+    late_sem=pltpu.SemaphoreType.DMA((8, 4)),
+    block_sem=pltpu.SemaphoreType.DMA((2, 4)),
 )
 SAVED = ("x", "q", "k", "v", "o", "h1", "q2", "k2", "v2", "o2", "h2", "sum1", "sum2", "sum3", "y")
-GATHER_ORDER = (0, 1, 2, 6, 4, 5, 3, 7, 8, 9, 10, 11, 12, 13, 14, 15)
-
-
-def weight_rows(refs, k, shard, start, size):
+GATHER_ORDER = (0, 1, 2, 6, 4, 5, 3, 7, 8, 12, 9, 13, 10, 14, 11, 15)
+AHEAD, HOPS = 3, (1, 2, 3)
+
+
+def weight_views(refs, k, shard, start, size):
     if k < 6:
-        return refs[0].at[k, rows_at(shard * 256 + start, size, 8), :]
+        return [refs[0].at[k, rows_at(shard * 256 + start, size, 8), :]]
     if k < 8:
-        return refs[1].at[k - 6, rows_at(shard * 256 + start, size, 8), :]
+        return [refs[1].at[k - 6, rows_at(shard * 256 + start, size, 8), :]]
     if k < 12:
-        return refs[2].at[rows_at(shard * 256 + (k - 8) * 64 + start, size, 8), :]
-    return refs[3].at[rows_at(shard * 1024 + (k - 12) * 256 + start, size, 8), :]
+        rows = rows_at(shard * 256 + start, size, 8)
+        return [refs[2].at[rows, pl.ds(i * 1024 + (k - 8) * 256, 256)] for i in range(4)]
+    return [refs[3].at[rows_at(shard * 1024 + (k - 12) * 256 + start, size, 8), :]]
 
 
 class Gatherer:
     def __init__(self, s, shards, full):
-        self.s, self.shards, self.full, self.done = s, shards, full, -4
+        self.s, self.shards, self.full, self.done = s, shards, full, -AHEAD - 1
         z, y, x, c = self.at = place()
         self.side = lax.rem(z, 2)
         self.core = device(z, y, x, 1 - c)
@@ -944,78 +952,77 @@
     def greet(self):
         greet([self.core, self.xmate, self.diag, self.ymate, self.zmate])
 
-    def size(self, k):
-        return 64 if 8 <= k < 12 else 256
+    def send(self, k, sources, target_shard, start, size, send, recv, peer):
+        targets = weight_views(self.full, k, target_shard, start, size)
+        return [
+            remote(src, dst, send.at[i], recv.at[i], peer)
+            for i, (src, dst) in enumerate(zip(sources, targets))
+        ]
 
     def x_copy(self, k):
-        n = self.size(k) // 4
-        q = (self.at[1] * 2 + self.side) * n
-        return remote(
-            weight_rows(self.shards, k, 0, q, n), weight_rows(self.full, k, self.mine, q, n),
+        q = (self.at[1] * 2 + self.side) * 64
+        return self.send(
+            k, weight_views(self.shards, k, 0, q, 64), self.mine, q, 64,
             self.s.x_send.at[k], self.s.x_recv.at[k], self.xmate,
         )
 
     def core_copy(self, k):
-        return remote(
-            weight_rows(self.shards, k, 0, 0, self.size(k)), weight_rows(self.full, k, self.mine, 0, self.size(k)),
+        return self.send(
+            k, weight_views(self.shards, k, 0, 0, 256), self.mine, 0, 256,
             self.s.c_send.at[k, 0], self.s.c_recv.at[k, 0], self.core,
         )
 
     def own_copy(self, k):
-        return pltpu.make_async_copy(
-            weight_rows(self.shards, k, 0, 0, self.size(k)), weight_rows(self.full, k, self.mine, 0, self.size(k)),
-            self.s.own_sem.at[k],
+        pairs = zip(weight_views(self.shards, k, 0, 0, 256), weight_views(self.full, k, self.mine, 0, 256))
+        return [
+            pltpu.make_async_copy(src, dst, self.s.own_sem.at[k, i]) for i, (src, dst) in enumerate(pairs)
+        ]
+
+    def relay(self, k, start, size, send, recv, peer):
+        return self.send(k, weight_views(self.full, k, self.other, start, size), self.other, start, size, send, recv, peer)
+
+    def first_hops(self, k):
+        s, q = self.s, (self.at[1] * 2 + self.side) * 64
+        return self.relay(k, q, 64, s.y_send.at[k, 0], s.y_recv.at[k, 0], self.ymate) + self.relay(
+            k, q, 64, s.z_send.at[k, 0], s.z_recv.at[k, 0], self.zmate
         )
 
-    def relay(self, k, start, n, send, recv, peer):
-        view = weight_rows(self.full, k, self.other, start, n)
-        return remote(view, view, send, recv, peer)
-
-    def first_hops(self, k):
-        s, n = self.s, self.size(k) // 4
-        q = (self.at[1] * 2 + self.side) * n
-        return [
-            self.relay(k, q, n, s.y_send.at[k, 0], s.y_recv.at[k, 0], self.ymate),
-            self.relay(k, q, n, s.z_send.at[k, 0], s.z_recv.at[k, 0], self.zmate),
-        ]
-
     def second_hops(self, k):
-        s, n, y = self.s, self.size(k) // 4, self.at[1]
-        return [
-            self.relay(k, (y * 2 + 1 - self.side) * n, n // 2, s.y_send.at[k, 1], s.y_recv.at[k, 1], self.ymate),
-            self.relay(
-                k, ((1 - y) * 2 + self.side) * n + n // 2, n // 2, s.z_send.at[k, 1], s.z_recv.at[k, 1], self.zmate
-            ),
-        ]
+        s, y = self.s, self.at[1]
+        return self.relay(
+            k, (y * 2 + 1 - self.side) * 64, 32, s.y_send.at[k, 1], s.y_recv.at[k, 1], self.ymate
+        ) + self.relay(
+            k, ((1 - y) * 2 + self.side) * 64 + 32, 32, s.z_send.at[k, 1], s.z_recv.at[k, 1], self.zmate
+        )
 
     def last_hop(self, k):
-        return self.relay(k, 0, self.size(k), self.s.c_send.at[k, 1], self.s.c_recv.at[k, 1], self.core)
+        return self.relay(k, 0, 256, self.s.c_send.at[k, 1], self.s.c_recv.at[k, 1], self.core)
 
     def step(self, t):
         def chunk(lag):
             return GATHER_ORDER[t - lag] if 0 <= t - lag < 16 else None
 
-        if (k := chunk(-3)) is not None:
-            self.x_copy(k).start()
-            self.core_copy(k).start()
-            self.own_copy(k).start()
+        def start(copies):
+            for copy in copies:
+                copy.start()
+
+        def wait(copies):
+            for copy in copies:
+                copy.wait()
+
+        if (k := chunk(-AHEAD)) is not None:
+            start(self.x_copy(k) + self.core_copy(k) + self.own_copy(k))
         if (k := chunk(0)) is not None:
-            self.x_copy(k).wait()
-            for copy in self.first_hops(k):
-                copy.start()
-        if (k := chunk(1)) is not None:
-            for copy in self.first_hops(k):
-                copy.wait()
-            for copy in self.second_hops(k):
-                copy.start()
-        if (k := chunk(2)) is not None:
-            for copy in self.second_hops(k):
-                copy.wait()
-            self.last_hop(k).start()
-        if (k := chunk(3)) is not None:
-            self.last_hop(k).wait()
-            self.core_copy(k).wait()
-            self.own_copy(k).wait()
+            wait(self.x_copy(k))
+            start(self.first_hops(k))
+        if (k := chunk(HOPS[0])) is not None:
+            wait(self.first_hops(k))
+            start(self.second_hops(k))
+        if (k := chunk(HOPS[1])) is not None:
+            wait(self.second_hops(k))
+            start(self.last_hop(k))
+        if (k := chunk(HOPS[2])) is not None:
+            wait(self.last_hop(k) + self.core_copy(k) + self.own_copy(k))
 
     def advance(self, t):
         while self.done < t:
@@ -1023,7 +1030,7 @@
             self.step(self.done)
 
     def ready(self, index):
-        self.advance(index + 3)
+        self.advance(index + HOPS[2])
 
 
 def forward_kernel(*refs):
@@ -1081,7 +1088,7 @@
         small[12 + i:13 + i, :] = up_bias[:, i * 256:(i + 1) * 256].astype(F32)
     small[16:17, :] = down_bias[...].astype(F32)
     gather.greet()
-    gather.advance(-2)
+    gather.advance(1 - AHEAD)
     for copy in token_copies():
         copy.start()
 
@@ -1095,9 +1102,13 @@
             return [pltpu.make_async_copy(s.v_out.at[k - 6], f_out.at[k - 6], s.weight_sem.at[k])]
         if k == 11:
             return [pltpu.make_async_copy(s.v_up, f_up, s.weight_sem.at[k])]
-        if k == 15:
-            return [pltpu.make_async_copy(s.v_down, f_down, s.weight_sem.at[k])]
-        return []
+        return [
+            pltpu.make_async_copy(src, dst, s.late_sem.at[k - 8, i])
+            for i, (src, dst) in enumerate(zip(late_views(full, k), late_views((f_in, f_out, f_up, f_down), k)))
+        ] if k > 11 else []
+
+    def late_views(refs, k):
+        return [view for shard in range(4) for view in weight_views(refs, k, shard, 0, 256)]
 
     def ready(index):
         gather.ready(index)
@@ -1184,7 +1195,7 @@
     save("v", s.v).start()
     for part in range(4):
         loop(2, lambda i, part=part: attend_pair(part * 2 + i, s.q, s.k, s.v, s.o, 512, True))
-        gather.advance(6 + part)
+        gather.advance(HOPS[2] + 3 + part // 2)
     save("o", s.o).start()
     ready(3)
     join(s.sum_a, s.x, s.o, s.v_out.at[0], 2)
@@ -1204,11 +1215,11 @@
     ready(7)
     for part in range(4):
         loop(2, lambda i, part=part: attend_pair(part * 2 + i, s.q2, s.k2, s.v2, s.o2, 256, False))
-        gather.advance(11 + part // 2)
+        gather.advance(HOPS[2] + 8 + part // 2)
     save("o2", s.o2).start()
     join(s.sum_b, s.hf, s.o2, s.v_out.at[1], 5)
     save("sum2", s.sum_b).start()
-    ready(10)
+    gather.advance(HOPS[2] + 9)
     normalize(s.sum_b, 1, s.h2, False)
     save("h2", s.h2).start()
     arrange(cot_in, s.s_tok)
@@ -1221,57 +1232,64 @@
         s.sum_a[p, :] = s.hf[p, :] + s.vec[16:17, :]
 
     loop(8, widen)
-    ready(11)
-
-    def block_copies(j, i, slot):
-        columns = rows_at(i * 1024 + j * 256, 256, 256)
-        return [
-            pltpu.make_async_copy(s.gblock.at[slot], g_all.at[:, columns], s.block_sem.at[slot, 0]),
-            pltpu.make_async_copy(s.dblock.at[slot], d_all.at[:, columns], s.block_sem.at[slot, 1]),
-        ]
+
+    def nudge():
+        gather.advance(min(gather.done + 1, 15 + HOPS[2]))
+
+    def block_copies(j, pair):
+        copies = []
+        for h in (0, 1):
+            columns = rows_at((2 * pair + h) * 1024 + j * 256, 256, 256)
+            part = pl.ds(h * 256, 256)
+            copies += [
+                pltpu.make_async_copy(s.gblock.at[pair, :, part], g_all.at[:, columns], s.block_sem.at[pair, h]),
+                pltpu.make_async_copy(s.dblock.at[pair, :, part], d_all.at[:, columns], s.block_sem.at[pair, 2 + h]),
+            ]
+        return copies
 
     for j in range(4):
-        ready(12 + j)
-
-        def mlp(i, j=j):
-            slot = lax.rem(i, 2)
-            columns = rows_at(i * 1024 + j * 256, 256, 256)
+        ready(8 + 2 * j)
+        ready(9 + 2 * j)
+
+        def mlp(pair, j=j):
             if j > 0:
-                for copy in block_copies(j, i, slot):
+                for copy in block_copies(j, pair):
                     copy.wait()
-            else:
-                @pl.when(i >= 2)
-                def _():
-                    for copy in block_copies(j, i, slot):
-                        copy.wait()
-
-            s.ublock[...] = dot_nn(s.h2[...], s.v_up[:, columns])
-            bias = s.v_small[i, 12 + j:13 + j, :]
+            starts = [(2 * pair + h) * 1024 + j * 256 for h in (0, 1)]
+            for h in (0, 1):
+                s.ublock[:, h * 256:(h + 1) * 256] = (
+                    dot_nn(s.h2[...], s.v_up[:, rows_at(starts[h], 256, 256)])
+                    + s.v_small[2 * pair + h, 12 + j:13 + j, :]
+                )
 
             def hidden(r):
                 p = rows_at(r * 64, 64, 64)
-                value = s.ublock[p, :] + bias
+                value = s.ublock[p, :]
                 cdf = normal_cdf(value)
                 pdf = jnp.exp(-0.5 * value * value) * 0.3989422804014327
-                s.gblock[slot, p, :] = (value * cdf).astype(BF16)
-                s.dblock[slot, p, :] = cdf + value * pdf
-
+                s.gblock[pair, p, :] = (value * cdf).astype(BF16)
+                s.dblock[pair, p, :] = cdf + value * pdf
+
+            nudge()
             loop(8, hidden)
-            for copy in block_copies(j, i, slot):
+            for copy in block_copies(j, pair):
                 copy.start()
 
             def out(n):
                 wide = rows_at(n * 256, 256, 256)
-                s.sum_a[:, wide] += dot_nn(s.gblock[slot], s.v_down[columns, wide])
+                s.sum_a[:, wide] += dot_nn(
+                    s.gblock[pair, :, 0:256], s.v_down[rows_at(starts[0], 256, 256), wide]
+                ) + dot_nn(s.gblock[pair, :, 256:512], s.v_down[rows_at(starts[1], 256, 256), wide])
 
             loop(4, out)
 
-        loop(4, mlp)
+        for pair in (0, 1):
+            mlp(pair)
 
     save("sum3", s.sum_a).start()
     normalize(s.sum_a, 2, s.y, True)
     save("y", s.y).start()
-    for copy in block_copies(3, 2, 0) + block_copies(3, 3, 1) + cot_copies():
+    for copy in block_copies(3, 0) + block_copies(3, 1) + cot_copies():
         copy.wait()
     for k in range(16):
         for copy in weight_saves(k):

time: 402 us -> 393 us (0.978)
  Pallas kernels: 398 us -> 387 us
    pallas_call x1, Pallas kernels: 139 us -> 132 us  [forward(): pl.pallas_call(forward_kernel, out_shape=(jax.ShapeDtypeStruct((6, 1024,...]
    pallas_call x1, Pallas kernels: 248 us -> 244 us  [backward(): pl.pallas_call(back_kernel, out_shape=(jax.ShapeDtypeStruct((CHUNKS, ROWS...]
where the time goes in v3:
time: 393 us; the launch traced here: 391 us
  Pallas kernels  387 us (98%)
    pallas_call x1, Pallas kernels, backward(): pl.pallas_call(back_kernel, out_shape=(jax.ShapeDtypeStruct((CHUNKS, ROWS...  244 us
    pallas_call x1, Pallas kernels, forward(): pl.pallas_call(forward_kernel, out_shape=(jax.ShapeDtypeStruct((6, 1024,...  132 us
    pallas_call x1, Pallas kernels, finish(): pl.pallas_call(finish_kernel, out_shape=tuple([jax.ShapeDtypeStruct((4, 1...  11.3 us

profile of v3, /device:TPU:0, one launch (start us, length us, event | category | flops | bytes accessed | tf_op | source)
XLA Modules:
  0.0 391.3 jit_solution(13038262866975788866)
XLA Ops:
  0.6 1.2 reshape.40.refs_6_
  1.9 1.3 reshape.39.refs_5_
  3.1 132.1 %shard_map.229 = (bf16[6,1024,1024]{2,1,0:T(8,128)(2,1)}, bf16[2,1024,1024]{2,1,0:T(8,128)(2,1)}, bf16[1024,4096]{1,0:T(8,128)(2,1)}, bf16[4096,1024]{1,0:T(8,12...) custom-call(s32[1,4]{1,0:T(1,128)} %owner.1, ...), custom_call_target="tpu_custom_call" | custom-call | tf_op jit(solution)/shard_map/pallas_call | solution.py:1310
  135.3 243.9 %shard_map.230 = (bf16[32,128,1024]{2,1,0:T(8,128)(2,1)}, f32[24,256]{1,0:T(8,128)}, bf16[256,1024]{1,0:T(8,128)(2,1)}, bf16[4,128,1024]{2,1,0:T(8,128)(2,1)}, b...) custom-call(bf16[512,1024]{1,0:T(8,128)(2,1)} %get-tuple-element.52.refs_0_, ...), custom_call_target="tpu_custom_call" | custom-call | tf_op jit(solution)/shard_map/pallas_call | solution.py:860
  379.2 0.0 copy-start
  379.2 11.3 %shard_map.231 = (bf16[4,128,1024]{2,1,0:T(8,128)(2,1)}, bf16[4,128,1024]{2,1,0:T(8,128)(2,1)}, f32[6,256,1024]{2,1,0:T(8,128)}, f32[2,256,1024]{2,1,0:T(8,128)}...) custom-call(s32[1,4]{1,0:T(1,128)} %owner.1, ...), custom_call_target="tpu_custom_call" | custom-call | tf_op jit(solution)/shard_map/pallas_call | solution.py:1405
  390.5 0.0 copy-done
  390.5 0.8 copy.27
Async XLA Ops:
  379.2 11.3 %copy-start = (bf16[256,1024]{1,0:T(8,128)(2,1)S(1)}, bf16[256,1024]{1,0:T(8,128)(2,1)}, u32[]{:S(2)}) copy-start(bf16[256,1024]{1,0:T(8,128)(2,1)} %get-tuple-element.82) | copy-start | bytes 1572868

commit v4 on v3

--- a/solution.py
+++ b/solution.py
@@ -1197,6 +1197,9 @@
         loop(2, lambda i, part=part: attend_pair(part * 2 + i, s.q, s.k, s.v, s.o, 512, True))
         gather.advance(HOPS[2] + 3 + part // 2)
     save("o", s.o).start()
+    arrange(cot_in, s.s_tok)
+    for copy in cot_copies():
+        copy.start()
     ready(3)
     join(s.sum_a, s.x, s.o, s.v_out.at[0], 2)
     save("sum1", s.sum_a).start()
@@ -1222,9 +1225,6 @@
     gather.advance(HOPS[2] + 9)
     normalize(s.sum_b, 1, s.h2, False)
     save("h2", s.h2).start()
-    arrange(cot_in, s.s_tok)
-    for copy in cot_copies():
-        copy.start()
     save("sum1", s.sum_a).wait()
 
     def widen(i):
@@ -1270,8 +1270,9 @@
                 s.gblock[pair, p, :] = (value * cdf).astype(BF16)
                 s.dblock[pair, p, :] = cdf + value * pdf
 
+            loop(4, hidden)
             nudge()
-            loop(8, hidden)
+            loop(4, lambda r: hidden(r + 4))
             for copy in block_copies(j, pair):
                 copy.start()
 

time: 393 us -> 400 us (1.018); the launches traced: 391 us -> 392 us
  no operation moved by 1% of the time
where the time goes in v4:
time: 400 us; the launch traced here: 392 us
  Pallas kernels  388 us (97%)
    pallas_call x1, Pallas kernels, backward(): pl.pallas_call(back_kernel, out_shape=(jax.ShapeDtypeStruct((CHUNKS, ROWS...  245 us
    pallas_call x1, Pallas kernels, forward(): pl.pallas_call(forward_kernel, out_shape=(jax.ShapeDtypeStruct((6, 1024,...  132 us
    pallas_call x1, Pallas kernels, finish(): pl.pallas_call(finish_kernel, out_shape=tuple([jax.ShapeDtypeStruct((4, 1...  11.3 us

profile of v4, /device:TPU:0, one launch (start us, length us, event | category | flops | bytes accessed | tf_op | source)
XLA Modules:
  0.0 392.2 jit_solution(13598141070183326428)
XLA Ops:
  0.6 1.2 reshape.40.refs_6_
  1.9 1.3 reshape.39.refs_5_
  3.1 131.8 %shard_map.229 = (bf16[6,1024,1024]{2,1,0:T(8,128)(2,1)}, bf16[2,1024,1024]{2,1,0:T(8,128)(2,1)}, bf16[1024,4096]{1,0:T(8,128)(2,1)}, bf16[4096,1024]{1,0:T(8,12...) custom-call(s32[1,4]{1,0:T(1,128)} %owner.1, ...), custom_call_target="tpu_custom_call" | custom-call | tf_op jit(solution)/shard_map/pallas_call | solution.py:1311
  134.9 244.7 %shard_map.230 = (bf16[32,128,1024]{2,1,0:T(8,128)(2,1)}, f32[24,256]{1,0:T(8,128)}, bf16[256,1024]{1,0:T(8,128)(2,1)}, bf16[4,128,1024]{2,1,0:T(8,128)(2,1)}, b...) custom-call(bf16[512,1024]{1,0:T(8,128)(2,1)} %get-tuple-element.52.refs_0_, ...), custom_call_target="tpu_custom_call" | custom-call | tf_op jit(solution)/shard_map/pallas_call | solution.py:860
  379.7 0.0 copy-start
  379.7 11.3 %shard_map.231 = (bf16[4,128,1024]{2,1,0:T(8,128)(2,1)}, bf16[4,128,1024]{2,1,0:T(8,128)(2,1)}, f32[6,256,1024]{2,1,0:T(8,128)}, f32[2,256,1024]{2,1,0:T(8,128)}...) custom-call(s32[1,4]{1,0:T(1,128)} %owner.1, ...), custom_call_target="tpu_custom_call" | custom-call | tf_op jit(solution)/shard_map/pallas_call | solution.py:1406
  391.0 0.0 copy-done
  391.0 0.8 copy.27
Async XLA Ops:
  379.7 11.3 %copy-start = (bf16[256,1024]{1,0:T(8,128)(2,1)S(1)}, bf16[256,1024]{1,0:T(8,128)(2,1)}, u32[]{:S(2)}) copy-start(bf16[256,1024]{1,0:T(8,128)(2,1)} %get-tuple-element.82) | copy-start | bytes 1572868
